TPU v7x, 128 devices: a whole 4x4x4 slice. The times are simulated.
128 devices in a mesh: grp: 16 (over z, x), reg: 8 (over y, core).
Axes of the slice: x: 4, y: 4, z: 4, core: 2. Of those that a mesh axis runs over, the one named last changes fastest.
Arguments:
- orbitals: bfloat16 [8, 16, 512, 1024], P('reg', 'grp'), may hold values from -6 to 6
- occupied: bfloat16 [8, 16, 8, 512], P('reg', 'grp'), may hold values from -0.59765625 to 0.59765625
- panel_index: int32 [128], replicated, may hold values from 0 to 1023, as said below
- screening: bfloat16 [896, 512, 512], P(('grp', 'reg')), may hold values from -0.25 to 0.25
- block_region: int32 [896, 1], P(('grp', 'reg')), may hold values from 0 to 7; in each aligned block of 7 rows (0 to 6, 7 to 13, ...) at most 2 rows name the same one
- block_row: int32 [896], P(('grp', 'reg')), may hold values from 0 to 15
- block_col: int32 [896], P(('grp', 'reg')), may hold values from 0 to 15
Outputs:
- sigma: float32 [8, 128, 128], P('reg')
Inputs may be any that keep to these rules, and one draw needn't show every extreme that they name: `panel_index`: the 128 indices are distinct. Among the 7 blocks of one device (aligned rows of block_region), at most 2 name the same region.
All inputs are finite; a program needn't handle non-finite values.
Results may differ from a plain program's by a relative error of at most 0.0054.
Values may be sent and summed in bfloat16 or wider, within the bound.
A program may use at most 192 MiB of HBM per device.

v0:
```python
import jax
import jax.numpy as jnp
from jax import lax
from jax.sharding import PartitionSpec as P

CAP = 2


def form_pairs(orbital_rows, occupied_rows):
    pairs = orbital_rows[..., :, None, :].astype(jnp.float32) * jnp.swapaxes(occupied_rows, -1, -2)[
        ..., None
    ].astype(jnp.float32)
    return pairs.astype(jnp.bfloat16)


def shards(orbitals, occupied, panel_index, screening, block_region, block_row, block_col):
    regions = lax.axis_size("reg")
    panel_orbs = jnp.take(orbitals[0], panel_index, axis=2)
    occ_rows = occupied[0]
    grid_points = screening.shape[1]
    panel_width = panel_orbs.shape[2]
    occ_count = occ_rows.shape[1]
    held_count = screening.shape[0]
    slot_count = regions * CAP
    destination = block_region[:, 0]
    membership = (destination[:, None] == jnp.arange(regions, dtype=jnp.int32)[None, :]).astype(
        jnp.int32
    )
    earlier = jnp.cumsum(membership, axis=0) - membership
    slot_of = destination * CAP + jnp.sum(earlier * membership, axis=1)
    matched = (slot_of[None, :] == jnp.arange(slot_count, dtype=jnp.int32)[:, None]).astype(
        jnp.int32
    )
    filled = jnp.sum(matched, axis=1)
    source = jnp.sum(matched * jnp.arange(held_count, dtype=jnp.int32)[None, :], axis=1)
    outgoing = jnp.take(screening, source, axis=0) * filled[:, None, None].astype(jnp.bfloat16)
    labels = jnp.stack(
        [jnp.take(block_row, source) * filled, jnp.take(block_col, source) * filled, filled], axis=1
    )
    gathered = lax.all_gather(form_pairs(panel_orbs, occ_rows), "grp", axis=0, tiled=True)

    def select_pairs(indices):
        return jnp.take(gathered, indices, axis=0)

    incoming, arrived = (
        lax.all_to_all(
            outgoing.reshape(regions, CAP, grid_points, grid_points),
            "reg",
            split_axis=0,
            concat_axis=0,
            tiled=True,
        ),
        lax.all_to_all(
            labels.reshape(regions, CAP, 3), "reg", split_axis=0, concat_axis=0, tiled=True
        ),
    )
    incoming = incoming.reshape(slot_count, grid_points, grid_points)
    arrived = arrived.reshape(slot_count, 3)
    col_pairs = select_pairs(arrived[:, 1]).reshape(
        slot_count, grid_points, occ_count * panel_width
    )
    screened = jnp.einsum(
        "spq,sqc->spc", incoming, col_pairs, preferred_element_type=jnp.float32
    ).astype(jnp.bfloat16)
    row_pairs = select_pairs(arrived[:, 0]).reshape(
        slot_count, grid_points * occ_count, panel_width
    )
    partial_sigma = jnp.einsum(
        "sri,srj->ij",
        row_pairs,
        screened.reshape(slot_count, grid_points * occ_count, panel_width),
        preferred_element_type=jnp.float32,
    )
    sigma = lax.psum(partial_sigma, "grp")
    return sigma[None]


def solution(mesh):
    in_specs = (
        P("reg", "grp", None, None),
        P("reg", "grp", None, None),
        P(),
        P(("grp", "reg"), None, None),
        P(("grp", "reg"), None),
        P(("grp", "reg")),
        P(("grp", "reg")),
    )
    out_specs = P("reg", None, None)
    return jax.shard_map(shards, mesh=mesh, in_specs=in_specs, out_specs=out_specs, check_vma=False)
```

profile of v0, /device:TPU:0, one launch (start us, length us, event | category | flops | bytes accessed | tf_op | source)
XLA Modules:
  0.0 339.6 jit_solution(4951172310689396512)
XLA Ops:
  6.5 0.7 compare_and_fusion.4
  7.9 0.7 convert_bitcast_fusion.1
  8.7 1.5 copy.26
  10.2 0.8 gather_fusion
  11.3 1.6 multiply_convert_fusion
  12.9 0.7 fusion.8
  13.6 0.8 select_reduce_fusion.1
  14.5 0.7 multiply_add_fusion
  15.9 1.3 gather_fusion.2
  17.5 0.7 copy.24
  18.2 4.6 %all-to-all-start = ((s32[8,2,3]{2,1,0:T(2,128)}), s32[8,2,3]{2,1,0:T(2,128)S(1)}, u32[]{:S(2)}, u32[]{:S(2)}) async-start(s32[8,2,3]{2,1,0:T(2,128)} %copy.24), calls=%async_computation | async-start | bytes 16384 | tf_op jit(solution)/shard_map/all_to_all | solution.py:53
  23.0 6.9 %gather_fusion.1 = bf16[16,512,512]{2,1,0:T(8,128)(2,1)} fusion(bf16[7,512,512]{2,1,0:T(8,128)(2,1)} %param.14, s32[1024]{0:T(1024)S(1)} %pad_clamp_fusion.1), kind=kCustom, calls=%fused_computation.5 | custom fusion | bytes 16777280 | tf_op jit(solution)/shard_map/jit(_take)/gather | solution.py:36
  29.9 7.4 %select_multiply_fusion = bf16[8,2,512,512]{3,2,1,0:T(8,128)(2,1)} fusion(bf16[8,2,512,512]{3,2,1,0:T(8,128)(2,1)} %bitcast.40, pred[8,2]{1,0:T(8,128)(4,1)S(1)} %compare_and_fusion, bf16[8,2]{1,0:T(8,128)(2,1)S(1)} %convert_element_type.65), kind=kLoop, calls=%fused_computation.13 | loop fusion | flops 8388608 | bytes 16777264 | tf_op jit(solution)/shard_map/mul | solution.py:36
  37.3 5.0 %all-to-all-start.1 = ((bf16[8,2,512,512]{3,2,1,0:T(8,128)(2,1)}), bf16[8,2,512,512]{3,2,1,0:T(8,128)(2,1)}, u32[]{:S(2)}, u32[]{:S(2)}) async-start(bf16[8,2,512,512]{3,2,1,0:T(8,128)(2,1)} %select_multiply_fusion), calls=%async_computation.1 | async-start | bytes 16777216 | tf_op jit(solution)/shard_map/all_to_all | solution.py:46
  42.8 84.2 %all-gather.2.cloned.1.call-done = bf16[16,512,8,128]{3,2,1,0:T(8,128)(2,1)} async-done(((bf16[1,512,8,128]{3,2,1,0:T(8,128)(2,1)}), bf16[16,512,8,128]{3,2,1,0:T(8,128)(2,1)}) %all-gather.2.cloned.1.call-update) | async-done | bytes 16777232 | tf_op jit(solution)/shard_map/all_gather | solution.py:40
  127.0 12.7 %gather_fusion.5 = bf16[16,512,8,128]{3,2,1,0:T(8,128)(2,1)} fusion(bf16[16,512,8,128]{3,2,1,0:T(8,128)(2,1)} %all-gather.2.cloned.1.call-done, s32[1024]{0:T(1024)S(1)} %pad_clamp_fusion), kind=kCustom, calls=%fused_computation.3.clone | custom fusion | bytes 33554496 | tf_op jit(solution)/shard_map/jit(_take)/gather | solution.py:43
  139.8 14.2 %broadcast_select_fusion = bf16[16,512,8,128]{3,2,1,0:T(8,128)(2,1)} fusion(bf16[16,512,8,128]{3,2,1,0:T(8,128)(2,1)} %gather_fusion.5, pred[16]{0:T(512)(128)(4,1)S(1)} %compare_and_fusion.1), kind=kLoop, calls=%fused_computation.9 | loop fusion | flops 8388608 | bytes 33554448 | tf_op jit(solution)/shard_map/jit(_take)/select_n | solution.py:43
  153.9 25.3 %reshape.130 = bf16[16,512,1024]{2,1,0:T(8,128)(2,1)} reshape(bf16[16,512,8,128]{3,2,1,0:T(8,128)(2,1)} %broadcast_select_fusion) | data formatting | bytes 33554432 | tf_op jit(solution)/shard_map/reshape | solution.py:59
  179.2 17.0 %convolution_convert_fusion = bf16[16,512,1024]{2,1,0:T(8,128)(2,1)} fusion(bf16[16,512,512]{2,1,0:T(8,128)(2,1)} %bitcast.12, bf16[16,512,1024]{2,1,0:T(8,128)(2,1)} %reshape.130), kind=kOutput, calls=%fused_computation.11 | convolution fusion | flops 8598323200 | bytes 41943040 | tf_op jit(solution)/shard_map/spq,sqc->spc/dot_general | solution.py:62
  196.2 25.3 %reshape.131 = bf16[16,4096,128]{2,1,0:T(8,128)(2,1)} reshape(bf16[16,512,1024]{2,1,0:T(8,128)(2,1)} %convolution_convert_fusion) | data formatting | bytes 33554432 | tf_op jit(solution)/shard_map/reshape | solution.py:71
  221.5 12.7 %gather_fusion.4 = bf16[16,512,8,128]{3,2,1,0:T(8,128)(2,1)} fusion(bf16[16,512,8,128]{3,2,1,0:T(8,128)(2,1)} %all-gather.2.cloned.1.call-done, s32[1024]{0:T(1024)S(1)} %pad_clamp_fusion.2), kind=kCustom, calls=%fused_computation.1.clone | custom fusion | bytes 33554496 | tf_op jit(solution)/shard_map/jit(_take)/gather | solution.py:43
  234.2 16.3 %fusion.5 = f32[1,128,128]{2,1,0:T(8,128)} fusion(bf16[16,4096,128]{2,1,0:T(8,128)(2,1)} %reshape.131, bf16[16,512,8,128]{3,2,1,0:T(8,128)(2,1)} %gather_fusion.4, pred[16]{0:T(512)(128)(4,1)S(1)} %compare_and_fusion.2), kind=kOutput, calls=%fused_computation.15 | convolution fusion | flops 2155872256 | bytes 33619984 | tf_op jit(solution)/shard_map/sri,srj->ij/dot_general | solution.py:68
  250.5 80.7 %all-reduce.2.cloned.1.call-done = f32[1,128,128]{2,1,0:T(8,128)} async-done(((f32[1,128,128]{2,1,0:T(8,128)}), f32[1,128,128]{2,1,0:T(8,128)}) %all-reduce.2.cloned.1.call-update) | async-done | bytes 65552 | tf_op jit(solution)/shard_map/psum | solution.py:74
  331.3 1.5 copy.35
  (39 shorter events, 2.8 us)
Async XLA Ops:
  6.5 8.7 %copy-start = (s32[7]{0:T(128)S(1)}, s32[7]{0:T(128)}, u32[]{:S(2)}) copy-start(s32[7]{0:T(128)} %param.17) | copy-start | bytes 88
  6.5 120.5 %all-gather.2.cloned.1.call-start = ((), (), s32[]{:S(2)}) async-start(), calls=%async_computation.2 | async-start | bytes 17825792 | tf_op jit(solution)/shard_map/all_gather | solution.py:40
  18.2 19.1 %all-to-all-start = ((s32[8,2,3]{2,1,0:T(2,128)}), s32[8,2,3]{2,1,0:T(2,128)S(1)}, u32[]{:S(2)}, u32[]{:S(2)}) async-start(s32[8,2,3]{2,1,0:T(2,128)} %copy.24), calls=%async_computation | async-start | bytes 16384 | tf_op jit(solution)/shard_map/all_to_all | solution.py:53
  37.3 141.9 %all-to-all-start.1 = ((bf16[8,2,512,512]{3,2,1,0:T(8,128)(2,1)}), bf16[8,2,512,512]{3,2,1,0:T(8,128)(2,1)}, u32[]{:S(2)}, u32[]{:S(2)}) async-start(bf16[8,2,512,512]{3,2,1,0:T(8,128)(2,1)} %select_multiply_fusion), calls=%async_computation.1 | async-start | bytes 16777216 | tf_op jit(solution)/shard_map/all_to_all | solution.py:46
  42.3 289.0 %all-reduce.2.cloned.1.call-start = ((), (), s32[]{:S(2)}) async-start(), calls=%async_computation.3 | async-start | bytes 131072 | tf_op jit(solution)/shard_map/psum | solution.py:74
  221.5 111.3 %copy-start.1 = (s32[7]{0:T(128)S(1)}, s32[7]{0:T(128)}, u32[]{:S(2)}) copy-start(s32[7]{0:T(128)} %param.17) | copy-start | bytes 88
Sparse Core Ops, SparseCore 0:
  13.0 113.9 all-gather.1
  250.7 80.5 all-reduce.1
where the time goes:
time: 342 us; the launch traced here: 340 us
  waiting for transfers between devices  165 us (48%)
  local copies, waits for them, and re-layouts  90.4 us (26%)
  matrix products  33.3 us (10%)
  other arithmetic  27.7 us (8%)
  between operations  13.5 us (4%)
  starting transfers between devices  9.75 us (3%)
    all_gather x1, waiting for transfers between devices, shards(): lax.all_gather(form_pairs(panel_orbs, occ_rows), 'grp', axis=0, tiled=True)  84.2 us
    psum x1, waiting for transfers between devices, shards(): sigma = lax.psum(partial_sigma, 'grp')  80.7 us
    gather x2, local copies, waits for them, and re-layouts, select_pairs(): return jnp.take(gathered, indices, axis=0)  25.5 us
    reshape x1, local copies, waits for them, and re-layouts, shards(): select_pairs(arrived[:, 1])  25.3 us
    reshape x1, local copies, waits for them, and re-layouts, shards(): screened.reshape(slot_count, grid_points * occ_count, panel_width)  25.3 us
    dot_general x1, matrix products, shards(): jnp.einsum('spq,sqc->spc', incoming, col_pairs, preferred_element_type=jn...  17 us
    dot_general x1, matrix products, shards(): jnp.einsum('sri,srj->ij', row_pairs, screened.reshape(slot_count, grid_po...  16.3 us
    select_n x3, other arithmetic, select_pairs(): return jnp.take(gathered, indices, axis=0)  14.2 us
  transfers between devices with their start and end apart: 4, of which 2 were waited for; matrix products, arithmetic and copies ran while one was open for 21% of the time, Pallas kernels for 0%

commit v1 on v0

v1 whole, which is shorter than its diff:
```python
import functools

import jax
import jax.numpy as jnp
from jax import lax
from jax.experimental import pallas as pl
from jax.experimental.pallas import tpu as pltpu
from jax.sharding import PartitionSpec as P

MESH = pl.DeviceIdType.MESH
SIDE = 4
ORDERS = (("x", "y", "z"), ("y", "z", "x"), ("z", "x", "y"))
STEPS = (1, -1, 2)


def mod4(v):
    return lax.rem(v + 2 * SIDE, SIDE)


def kernel(
    slices,
    orb_ref,
    occ_ref,
    pidx_ref,
    w_hbm,
    region_ref,
    row_ref,
    col_ref,
    out_ref,
    b0,
    b1,
    b2,
    oc,
    wv,
    wg,
    acc,
    part,
    red,
    pieces,
    w_sem,
    p1s,
    p1r,
    p2s,
    p2r,
    p3s,
    p3r,
    d2s,
    d2r,
    os,
    orr,
    ods,
    odr,
    r1s,
    r1r,
    r2s,
    r2r,
    r3s,
    r3r,
):
    bufs = (b0, b1, b2)
    held = w_hbm.shape[0]
    points = w_hbm.shape[1]
    grp = lax.axis_index("grp")
    reg = lax.axis_index("reg")
    me = {"z": grp // SIDE, "x": lax.rem(grp, SIDE), "y": reg // 2}
    core = lax.rem(reg, 2)

    def device(z, x, y, c):
        return (mod4(z) * SIDE + mod4(x), mod4(y) * 2 + c)

    def near(axis, step):
        at = {k: me[k] + (step if k == axis else 0) for k in me}
        return device(at["z"], at["x"], at["y"], core)

    sibling = (grp, me["y"] * 2 + 1 - core)
    unsent = []

    def send(src, dst, ssem, rsem, to):
        copy = pltpu.make_async_remote_copy(src, dst, ssem, rsem, device_id=to, device_id_type=MESH)
        copy.start()
        unsent.append(copy)
        return copy

    barrier = pltpu.get_barrier_semaphore()
    partners = [near(axis, step) for axis in "xyz" for step in STEPS] + [sibling]
    for to in partners:
        pl.semaphore_signal(barrier, inc=1, device_id=to, device_id_type=MESH)

    w_copy = pltpu.make_async_copy(w_hbm, wv, w_sem)
    w_copy.start()

    orbs = orb_ref.shape[3]
    width = pidx_ref.shape[1]
    chosen = (
        lax.broadcasted_iota(jnp.int32, (orbs, width), 0)
        == jnp.broadcast_to(pidx_ref[...], (orbs, width))
    ).astype(jnp.bfloat16)
    start = 0
    for s, buf in enumerate(bufs):
        a1, a2, a3 = ORDERS[s]
        rows = slices[s]
        buf[core, me[a3], me[a2], me[a1]] = jnp.dot(
            orb_ref[0, 0, start : start + rows, :], chosen, preferred_element_type=jnp.float32
        ).astype(jnp.bfloat16)
        start += rows
    oc[core, me["z"], me["y"], me["x"]] = occ_ref[0, 0]

    pl.semaphore_wait(barrier, len(partners))

    def occ_step(phase):
        axis = "xyz"[phase]
        at = (core, me["z"], me["y"], me["x"])[: 4 - phase]
        block = oc.at[at]
        return [
            send(block, block, os.at[phase, i], orr.at[phase, i], near(axis, step))
            for i, step in enumerate(STEPS)
        ]

    occ_sent = occ_step(0)
    first = []
    for s, buf in enumerate(bufs):
        a1, a2, a3 = ORDERS[s]
        block = buf.at[core, me[a3], me[a2], me[a1]]
        first.append(
            [
                send(block, block, p1s.at[s, i], p1r.at[s, i], near(a1, step))
                for i, step in enumerate(STEPS)
            ]
        )

    def both(block, ssem, rsem, axis):
        return [
            send(block, block, ssem.at[i], rsem.at[i], near(axis, step))
            for i, step in enumerate((1, -1))
        ]

    mirrored = []

    def mirror(s, i3, i2, slot):
        block = bufs[s].at[core, i3, i2]
        mirrored.append(send(block, block, d2s.at[s, slot], d2r.at[s, slot], sibling))

    for copy in occ_sent:
        copy.wait_recv()
    occ_sent = occ_step(1)

    second, third = [], [[], [], []]
    for s, buf in enumerate(bufs):
        a1, a2, a3 = ORDERS[s]
        for copy in first[s]:
            copy.wait_recv()
        block = buf.at[core, me[a3], me[a2]]
        second.append(both(block, p2s.at[s], p2r.at[s], a2))
        third[s].append(both(block, p3s.at[s, 0], p3r.at[s, 0], a3))
        mirror(s, me[a3], me[a2], 0)

    for copy in occ_sent:
        copy.wait_recv()
    occ_sent = occ_step(2)

    forwards = []
    for s, buf in enumerate(bufs):
        a1, a2, a3 = ORDERS[s]
        passed = []
        for i, step in enumerate((1, -1)):
            second[s][i].wait_recv()
            j = mod4(me[a2] - step)
            half = buf.at[core, me[a3], j, pl.ds(2 * i, 2)]
            passed.append(send(half, half, p2s.at[s, 2 + i], p2r.at[s, 2 + i], near(a2, step)))
            block = buf.at[core, me[a3], j]
            third[s].append(both(block, p3s.at[s, 1 + i], p3r.at[s, 1 + i], a3))
            mirror(s, me[a3], j, 1 + i)
        forwards.append(passed)
    for s, buf in enumerate(bufs):
        a1, a2, a3 = ORDERS[s]
        for copy in forwards[s]:
            copy.wait_recv()
        j = mod4(me[a2] + 2)
        block = buf.at[core, me[a3], j]
        third[s].append(both(block, p3s.at[s, 3], p3r.at[s, 3], a3))
        mirror(s, me[a3], j, 3)

    for copy in occ_sent:
        copy.wait_recv()
    occ_side = send(oc.at[core], oc.at[core], ods, odr, sibling)
    w_copy.wait()

    def place(n, ref):
        d, g = region_ref[n, 0], ref[n]
        return lax.rem(d, 2), {"y": d // 2, "z": g // SIDE, "x": lax.rem(g, SIDE)}

    def weigh(n, carry):
        ca, pa = place(n, row_ref)
        cb, pb = place(n, col_ref)
        occ_a = oc[ca, pa["z"], pa["y"], pa["x"]]
        occ_b = oc[cb, pb["z"], pb["y"], pb["x"]]
        gram = lax.dot_general(
            occ_a, occ_b, (((0,), (0,)), ((), ())), preferred_element_type=jnp.float32
        )
        wg[n] = (gram * wv[n].astype(jnp.float32)).astype(jnp.bfloat16)
        return carry

    last = []
    for k in range(4):
        passed = []
        for s, buf in enumerate(bufs):
            a1, a2, a3 = ORDERS[s]
            j = mod4(me[a2] + (0, -1, 1, 2)[k])
            pair = []
            for i, step in enumerate((1, -1)):
                third[s][k][i].wait_recv()
                i3 = mod4(me[a3] - step)
                half = buf.at[core, i3, j, pl.ds(2 * i, 2)]
                pair.append(
                    send(half, half, p3s.at[s, k, 2 + i], p3r.at[s, k, 2 + i], near(a3, step))
                )
                mirror(s, i3, j, 4 + 3 * k + i)
            passed.append(pair)
        last.append(passed)
        if k == 0:
            occ_side.wait_recv()
        low, high = 2 * k, min(2 * k + 2, held)
        lax.fori_loop(low, high, weigh, 0)
        if k >= 1:
            for s in range(3):
                a1, a2, a3 = ORDERS[s]
                for copy in last[k - 1][s]:
                    copy.wait_recv()
                mirror(s, mod4(me[a3] + 2), mod4(me[a2] + (0, -1, 1, 2)[k - 1]), 6 + 3 * (k - 1))
    for s in range(3):
        a1, a2, a3 = ORDERS[s]
        for copy in last[3][s]:
            copy.wait_recv()
        mirror(s, mod4(me[a3] + 2), mod4(me[a2] + 2), 15)
    for copy in mirrored:
        copy.wait_recv()

    acc[...] = jnp.zeros_like(acc)

    def whole(c, at):
        return jnp.concatenate(
            [bufs[s][c, at[a3], at[a2], at[a1]] for s, (a1, a2, a3) in enumerate(ORDERS)], axis=0
        )

    def contract(n, carry):
        ca, pa = place(n, row_ref)
        cb, pb = place(n, col_ref)
        screened = jnp.dot(
            wg[n], whole(cb, pb), preferred_element_type=jnp.float32
        ).astype(jnp.bfloat16)
        term = lax.dot_general(
            whole(ca, pa), screened, (((0,), (0,)), ((), ())), preferred_element_type=jnp.float32
        )
        for c in range(2):
            for y in range(SIDE):
                hit = region_ref[n, 0] == 2 * y + c
                acc[c, y] += jnp.where(hit, term, 0.0)
        return carry

    lax.fori_loop(0, held, contract, 0)

    swap = send(acc.at[1 - core], part, r1s, r1r, sibling)
    swap.wait_recv()
    red[...] = acc[core] + part[...]

    rows = pieces.shape[1]
    sums = []
    for k in range(1, 64):
        z, x, y = mod4(me["z"] + k // 16), mod4(me["x"] + (k // 4) % 4), mod4(me["y"] + k % 4)
        piece = red.at[y, pl.ds(pl.multiple_of((z * SIDE + x) * rows, rows), rows)]
        sums.append(send(piece, pieces.at[k], r2s.at[k], r2r.at[k], device(z, x, y, core)))
    mine = pl.ds(pl.multiple_of(grp * rows, rows), rows)
    total = red[me["y"], mine]
    for k in range(1, 64):
        sums[k - 1].wait_recv()
        total = total + pieces[k]
    out_ref[0, mine] = total
    done = []
    for k in range(1, 16):
        to = device(me["z"] + k // 4, me["x"] + k % 4, me["y"], core)
        done.append(send(out_ref.at[0, mine], out_ref.at[0, mine], r3s.at[k], r3r.at[k], to))
    for copy in done:
        copy.wait_recv()
    for copy in unsent:
        copy.wait_send()


def shards(orbitals, occupied, panel_index, screening, block_region, block_row, block_col):
    held, points = screening.shape[0], screening.shape[1]
    width = panel_index.shape[0]
    tiles = points // 16
    slices = [16 * (tiles * (s + 1) // 3 - tiles * s // 3) for s in range(3)]
    occ_count = occupied.shape[2]
    vmem = pl.BlockSpec(memory_space=pltpu.VMEM)
    smem = pl.BlockSpec(memory_space=pltpu.SMEM)
    dma = pltpu.SemaphoreType.DMA
    pairs = [dma((3, 3))] * 2 + [dma((3, 4))] * 2 + [dma((3, 4, 4))] * 2 + [dma((3, 16))] * 2
    pairs += [dma((3, 3))] * 2 + [dma] * 4 + [dma((64,))] * 2 + [dma((16,))] * 2
    return pl.pallas_call(
        functools.partial(kernel, slices),
        out_shape=jax.ShapeDtypeStruct((1, width, width), jnp.float32),
        in_specs=[vmem, vmem, vmem, pl.BlockSpec(memory_space=pl.ANY), smem, smem, smem],
        out_specs=vmem,
        scratch_shapes=[
            pltpu.VMEM((2, SIDE, SIDE, SIDE, rows, width), jnp.bfloat16) for rows in slices
        ]
        + [
            pltpu.VMEM((2, SIDE, SIDE, SIDE, occ_count, points), jnp.bfloat16),
            pltpu.VMEM((held, points, points), jnp.bfloat16),
            pltpu.VMEM((held, points, points), jnp.bfloat16),
            pltpu.VMEM((2, SIDE, width, width), jnp.float32),
            pltpu.VMEM((SIDE, width, width), jnp.float32),
            pltpu.VMEM((SIDE, width, width), jnp.float32),
            pltpu.VMEM((64, width // 16, width), jnp.float32),
            dma,
        ]
        + pairs,
        compiler_params=pltpu.CompilerParams(
            collective_id=0, has_side_effects=True, vmem_limit_bytes=56 * 2**20
        ),
    )(
        orbitals,
        occupied,
        panel_index.reshape(1, width),
        screening,
        block_region,
        block_row,
        block_col,
    )


def solution(mesh):
    in_specs = (
        P("reg", "grp", None, None),
        P("reg", "grp", None, None),
        P(),
        P(("grp", "reg"), None, None),
        P(("grp", "reg"), None),
        P(("grp", "reg")),
        P(("grp", "reg")),
    )
    out_specs = P("reg", None, None)
    return jax.shard_map(shards, mesh=mesh, in_specs=in_specs, out_specs=out_specs, check_vma=False)
```

time: 342 us -> 75.8 us (0.22)
  waiting for transfers between devices: 165 us -> 0 us
  local copies, waits for them, and re-layouts: 90.4 us -> 2.8 us
  Pallas kernels: 0 us -> 72.8 us
  matrix products: 33.3 us -> 0 us
  other arithmetic: 27.7 us -> 0 us
  between operations: 13.5 us -> 0.01 us
  starting transfers between devices: 9.75 us -> 0 us
    all_gather x1 -> x0, waiting for transfers between devices: 84.2 us -> none  [shards(): lax.all_gather(form_pairs(panel_orbs, occ_rows), 'grp', axis=0, tiled=True)]
    psum x1 -> x0, waiting for transfers between devices: 80.7 us -> none  [shards(): sigma = lax.psum(partial_sigma, 'grp')]
    pallas_call x0 -> x1, Pallas kernels: none -> 72.8 us  [shards(): pl.pallas_call(functools.partial(kernel, slices), out_shape=jax.ShapeDtyp...]
    reshape x2 -> x0, local copies, waits for them, and re-layouts: 50.6 us -> none  [the longest x1 25.3 us: shards(): select_pairs(arrived[:, 1])]
    gather x6 -> x0, local copies, waits for them, and re-layouts: 35.2 us -> none  [the longest x2 25.5 us: select_pairs(): return jnp.take(gathered, indices, axis=0)]
    dot_general x2 -> x0, matrix products: 33.3 us -> none  [the longest x1 17 us: shards(): jnp.einsum('spq,sqc->spc', incoming, col_pairs, preferred_element_type=jn...]
    select_n x6 -> x0, other arithmetic: 14.8 us -> none  [the longest x3 14.2 us: select_pairs(): return jnp.take(gathered, indices, axis=0)]
    all_to_all x2 -> x0, starting transfers between devices: 9.52 us -> none  [the longest x1 4.97 us: shards(): lax.all_to_all(outgoing.reshape(regions, CAP, grid_points, grid_points),...]
  transfers between devices with their start and end apart: 4 -> 0, of which waited for: 2 -> 0; matrix products, arithmetic and copies ran while one was open for 21% -> 0% of each run, Pallas kernels for 0% -> 0%
where the time goes in v1:
time: 75.8 us; the launch traced here: 75.6 us
  Pallas kernels  72.8 us (96%)
  local copies, waits for them, and re-layouts  2.8 us (4%)
    pallas_call x1, Pallas kernels, shards(): pl.pallas_call(functools.partial(kernel, slices), out_shape=jax.ShapeDtyp...  72.8 us
    unnamed x2, local copies, waits for them, and re-layouts  2.8 us

profile of v1, /device:TPU:0, one launch (start us, length us, event | category | flops | bytes accessed | tf_op | source)
XLA Modules:
  0.0 75.6 jit_solution(16760679375267500186)
XLA Ops:
  0.0 1.3 %copy.8.region_ref = s32[7,1]{1,0:T(8,128)} copy(s32[7,1]{0,1:T(1,128)} %param.11) | data formatting | bytes 56 | tf_op args[4]
  1.3 72.8 %shard_map.73 = f32[1,128,128]{2,1,0:T(8,128)} custom-call(bf16[1,1,512,1024]{3,2,1,0:T(8,128)(2,1)} %orb_ref.1, bf16[1,1,8,512]{3,2,1,0:T(8,128)(2,1)} %occ_ref.1, s32[1,128]{1,0:T(1,128)} %bitcast.1, bf16[7,512,512]{2,1,0:T(8,128)(2,1)} %w_hbm.1, s32[7,1]{1,0:T(8,128)} %copy.8.region_ref, s32[7]{0:T(128)} %row_ref.1, s32[7]{0:T(128)} %col_ref.1), custom_call_target="tpu_custom_call" | custom-call | tf_op jit(solution)/shard_map/pallas_call | solution.py:299
  74.1 1.5 %copy.10 = f32[1,128,128]{2,1,0:T(8,128)} copy(f32[1,128,128]{2,1,0:T(8,128)} %shard_map.73) | data formatting | bytes 131072

commit v2 on v0

v2 whole, which is shorter than its diff:
```python
import functools

import jax
import jax.numpy as jnp
from jax import lax
from jax.experimental import pallas as pl
from jax.experimental.pallas import tpu as pltpu
from jax.sharding import PartitionSpec as P

MESH = pl.DeviceIdType.MESH
SIDE = 4
ORDERS = (("x", "y", "z"), ("y", "z", "x"), ("z", "x", "y"))
STEPS = (1, -1, 2)
COPIES = 256


def mod4(v):
    return lax.rem(v + 2 * SIDE, SIDE)


def kernel(
    slices,
    orb_hbm,
    occ_hbm,
    pidx_hbm,
    w_hbm,
    region_hbm,
    row_hbm,
    col_hbm,
    out_ref,
    b0,
    b1,
    b2,
    oc,
    orb,
    pidx,
    wv,
    wg,
    acc,
    part,
    red,
    pieces,
    region,
    row,
    col,
    local_sem,
    send_sem,
    recv_sem,
):
    bufs = (b0, b1, b2)
    held = w_hbm.shape[0]
    grp = lax.axis_index("grp")
    reg = lax.axis_index("reg")
    me = {"z": grp // SIDE, "x": lax.rem(grp, SIDE), "y": reg // 2}
    core = lax.rem(reg, 2)

    def device(z, x, y, c):
        return (mod4(z) * SIDE + mod4(x), mod4(y) * 2 + c)

    def near(axis, step):
        at = {k: me[k] + (step if k == axis else 0) for k in me}
        return device(at["z"], at["x"], at["y"], core)

    sibling = (grp, me["y"] * 2 + 1 - core)
    sent = []

    def send(src, dst, to):
        n = len(sent)
        copy = pltpu.make_async_remote_copy(
            src, dst, send_sem.at[n], recv_sem.at[n], device_id=to, device_id_type=MESH
        )
        copy.start()
        sent.append(copy)
        return copy

    loads = [
        pltpu.make_async_copy(src, dst, local_sem.at[i])
        for i, (src, dst) in enumerate(
            [
                (pidx_hbm, pidx),
                (orb_hbm.at[0, 0], orb),
                (occ_hbm.at[0, 0], oc.at[0, 0, 0, 0]),
                (region_hbm, region),
                (row_hbm, row),
                (col_hbm, col),
                (w_hbm, wv),
            ]
        )
    ]
    for load in loads[:-1]:
        load.start()
    barrier = pltpu.get_barrier_semaphore()
    partners = [near(axis, step) for axis in "xyz" for step in STEPS] + [sibling]
    for to in partners:
        pl.semaphore_signal(barrier, inc=1, device_id=to, device_id_type=MESH)

    orbs = orb.shape[1]
    width = pidx.shape[1]
    loads[0].wait()
    chosen = (
        lax.broadcasted_iota(jnp.int32, (orbs, width), 0)
        == jnp.broadcast_to(pidx[...], (orbs, width))
    ).astype(jnp.bfloat16)
    loads[1].wait()
    start = 0
    for s, buf in enumerate(bufs):
        buf[0, 0, 0, 0] = jnp.dot(
            orb[start : start + slices[s], :], chosen, preferred_element_type=jnp.float32
        ).astype(jnp.bfloat16)
        start += slices[s]
    for load in loads[2:-1]:
        load.wait()
    pl.semaphore_wait(barrier, len(partners))

    def occ_step(phase):
        even, odd = "xyz"[phase], "zxy"[phase]
        copies = []
        for step in STEPS:
            at = {k: me[k] + step * ((1 - core) * (k == even) + core * (k == odd)) for k in me}
            inner = (0,) * (3 - phase)
            src = oc.at[inner + (0,)]
            dst = oc.at[inner + ((-step) % SIDE,)]
            copies.append(send(src, dst, device(at["z"], at["x"], at["y"], core)))
        return copies

    def ring(s, phase, units, *outer):
        buf, axis = bufs[s], ORDERS[s][phase - 1]
        copies = []
        for step in (1, -1):
            slot = (-step) % SIDE
            if phase == 2:
                src, dst = buf.at[0, 0, 0, units], buf.at[0, 0, slot, units]
            else:
                src, dst = buf.at[0, 0, outer[0], units], buf.at[0, slot, outer[0], units]
            copies.append(send(src, dst, near(axis, step)))
        return copies

    def pass_on(s, phase, side, units, *outer):
        buf, axis = bufs[s], ORDERS[s][phase - 1]
        step = (1, -1)[side]
        slot = (-step) % SIDE
        cut = 16 * ((slices[s] + 31) // 32)
        rows = pl.ds(0, cut) if side == 0 else pl.ds(cut, slices[s] - cut)
        if phase == 2:
            src, dst = buf.at[0, 0, slot, units, rows], buf.at[0, 0, 2, units, rows]
        else:
            src, dst = buf.at[0, slot, outer[0], units, rows], buf.at[0, 2, outer[0], units, rows]
        return send(src, dst, near(axis, step))

    mirrored = []

    def mirror(s, i3, i2):
        mirrored.append(send(bufs[s].at[0, i3, i2], bufs[s].at[1, i3, i2], sibling))

    def arrive(copies):
        for copy in copies:
            copy.wait_recv()

    own, rest, full = pl.ds(0, 1), pl.ds(1, 3), pl.ds(0, 4)
    each = range(3)

    occ_sent = occ_step(0)
    first = [
        [
            send(bufs[s].at[0, 0, 0, 0], bufs[s].at[0, 0, 0, (-step) % SIDE], near(ORDERS[s][0], step))
            for step in STEPS
        ]
        for s in each
    ]
    second_own = [ring(s, 2, own) for s in each]
    third_own = [ring(s, 3, own, 0) for s in each]
    loads[-1].start()

    arrive(occ_sent)
    occ_sent = occ_step(1)
    second_rest, third_rest = [], []
    for s in each:
        arrive(first[s])
        second_rest.append(ring(s, 2, rest))
        third_rest.append(ring(s, 3, rest, 0))
        mirror(s, 0, 0)
    arrive(occ_sent)
    occ_sent = occ_step(2)

    second_far, third_far = [[], [], []], [[], [], []]
    for s in each:
        for side in (0, 1):
            second_own[s][side].wait_recv()
            second_far[s].append(pass_on(s, 2, side, own))
            third_own[s][side].wait_recv()
            third_far[s].append(pass_on(s, 3, side, own, 0))

    third = [{}, {}, {}]
    for s in each:
        for side, slot in ((0, 3), (1, 1)):
            second_rest[s][side].wait_recv()
            second_far[s].append(pass_on(s, 2, side, rest))
            third[s][slot] = ring(s, 3, full, slot)
            mirror(s, 0, slot)
    for s in each:
        for side, slot in ((0, 3), (1, 1)):
            third_rest[s][side].wait_recv()
            third_far[s].append(pass_on(s, 3, side, rest, 0))
            mirror(s, slot, 0)
    for s in each:
        arrive(second_far[s])
        third[s][2] = ring(s, 3, full, 2)
        mirror(s, 0, 2)

    arrive(occ_sent)
    occ_side = send(oc.at[0], oc.at[1], sibling)
    loads[-1].wait()

    def place(n, ref):
        d, g = region[n], ref[n]
        parity = lax.rem(d, 2)
        at = {
            "y": mod4(d // 2 - me["y"]),
            "z": mod4(g // SIDE - me["z"]),
            "x": mod4(lax.rem(g, SIDE) - me["x"]),
        }
        return parity, lax.rem(parity + core, 2), at

    def occ_of(n, ref):
        parity, c, at = place(n, ref)
        x, y, z = at["x"], at["y"], at["z"]
        return oc[c, z + parity * (y - z), y + parity * (x - y), x + parity * (z - x)]

    def weigh(n, carry):
        gram = lax.dot_general(
            occ_of(n, row),
            occ_of(n, col),
            (((0,), (0,)), ((), ())),
            preferred_element_type=jnp.float32,
        )
        wg[n] = (gram * wv[n].astype(jnp.float32)).astype(jnp.bfloat16)
        return carry

    third_last = [[], [], []]
    for s in each:
        arrive(third_far[s])
        mirror(s, 2, 0)
    for k, j in enumerate((3, 1, 2)):
        for s in each:
            for side, slot in ((0, 3), (1, 1)):
                third[s][j][side].wait_recv()
                third_last[s].append(pass_on(s, 3, side, full, j))
                mirror(s, slot, j)
        if k == 0:
            occ_side.wait_recv()
        lax.fori_loop(3 * k, min(3 * k + 3, held), weigh, 0)
    for k, j in enumerate((3, 1, 2)):
        for s in each:
            arrive(third_last[s][2 * k : 2 * k + 2])
            mirror(s, 2, j)
    arrive(mirrored)

    acc[...] = jnp.zeros_like(acc)

    def whole(n, ref):
        _, c, at = place(n, ref)
        return jnp.concatenate(
            [bufs[s][c, at[a3], at[a2], at[a1]] for s, (a1, a2, a3) in enumerate(ORDERS)], axis=0
        )

    def contract(n, carry):
        screened = jnp.dot(
            wg[n], whole(n, col), preferred_element_type=jnp.float32
        ).astype(jnp.bfloat16)
        term = lax.dot_general(
            whole(n, row), screened, (((0,), (0,)), ((), ())), preferred_element_type=jnp.float32
        )
        for c in range(2):
            for y in range(SIDE):
                hit = region[n] == 2 * mod4(me["y"] + y) + lax.rem(core + c, 2)
                acc[c, y] += jnp.where(hit, term, 0.0)
        return carry

    lax.fori_loop(0, held, contract, 0)

    swaps = [send(acc.at[1, y], part.at[y], sibling) for y in range(SIDE)]
    rows = pieces.shape[1]
    sums = []
    for y in range(SIDE):
        swaps[y].wait_recv()
        red[y] = acc[0, y] + part[y]
        for k in range(y, 64, 4):
            if k:
                z, x = mod4(me["z"] + k // 16), mod4(me["x"] + (k // 4) % 4)
                piece = red.at[y, pl.ds(pl.multiple_of((z * SIDE + x) * rows, rows), rows)]
                sums.append(send(piece, pieces.at[k], device(z, x, me["y"] + y, core)))
    mine = pl.ds(pl.multiple_of(grp * rows, rows), rows)
    total = red[0, mine]
    arrive(sums)
    for k in range(1, 64):
        total = total + pieces[k]
    out_ref[0, mine] = total
    done = [
        send(
            out_ref.at[0, mine],
            out_ref.at[0, mine],
            device(me["z"] + k // 4, me["x"] + k % 4, me["y"], core),
        )
        for k in range(1, 16)
    ]
    arrive(done)
    for copy in sent:
        copy.wait_send()


def shards(orbitals, occupied, panel_index, screening, block_region, block_row, block_col):
    held, points = screening.shape[0], screening.shape[1]
    orbs = orbitals.shape[3]
    width = panel_index.shape[0]
    tiles = points // 16
    cuts = [0, tiles * 5 // 16, tiles * 11 // 16, tiles]
    slices = [16 * (cuts[s + 1] - cuts[s]) for s in range(3)]
    occ_count = occupied.shape[2]
    hbm = pl.BlockSpec(memory_space=pl.ANY)
    dma = pltpu.SemaphoreType.DMA
    return pl.pallas_call(
        functools.partial(kernel, slices),
        out_shape=jax.ShapeDtypeStruct((1, width, width), jnp.float32),
        in_specs=[hbm] * 7,
        out_specs=pl.BlockSpec(memory_space=pltpu.VMEM),
        scratch_shapes=[
            pltpu.VMEM((2, SIDE, SIDE, SIDE, rows, width), jnp.bfloat16) for rows in slices
        ]
        + [
            pltpu.VMEM((2, SIDE, SIDE, SIDE, occ_count, points), jnp.bfloat16),
            pltpu.VMEM((points, orbs), jnp.bfloat16),
            pltpu.VMEM((1, width), jnp.int32),
            pltpu.VMEM((held, points, points), jnp.bfloat16),
            pltpu.VMEM((held, points, points), jnp.bfloat16),
            pltpu.VMEM((2, SIDE, width, width), jnp.float32),
            pltpu.VMEM((SIDE, width, width), jnp.float32),
            pltpu.VMEM((SIDE, width, width), jnp.float32),
            pltpu.VMEM((64, width // 16, width), jnp.float32),
            pltpu.SMEM((held,), jnp.int32),
            pltpu.SMEM((held,), jnp.int32),
            pltpu.SMEM((held,), jnp.int32),
            dma((7,)),
            dma((COPIES,)),
            dma((COPIES,)),
        ],
        compiler_params=pltpu.CompilerParams(
            collective_id=0, has_side_effects=True, vmem_limit_bytes=56 * 2**20
        ),
    )(
        orbitals,
        occupied,
        panel_index.reshape(1, width),
        screening,
        block_region.reshape(held),
        block_row,
        block_col,
    )


def solution(mesh):
    in_specs = (
        P("reg", "grp", None, None),
        P("reg", "grp", None, None),
        P(),
        P(("grp", "reg"), None, None),
        P(("grp", "reg"), None),
        P(("grp", "reg")),
        P(("grp", "reg")),
    )
    out_specs = P("reg", None, None)
    return jax.shard_map(shards, mesh=mesh, in_specs=in_specs, out_specs=out_specs, check_vma=False)
```

time: 342 us -> 69.4 us (0.20)
  waiting for transfers between devices: 165 us -> 0 us
  local copies, waits for them, and re-layouts: 90.4 us -> 1.47 us
  Pallas kernels: 0 us -> 67.8 us
  matrix products: 33.3 us -> 0 us
  other arithmetic: 27.7 us -> 0 us
  between operations: 13.5 us -> 0.01 us
  starting transfers between devices: 9.75 us -> 0 us
    all_gather x1 -> x0, waiting for transfers between devices: 84.2 us -> none  [shards(): lax.all_gather(form_pairs(panel_orbs, occ_rows), 'grp', axis=0, tiled=True)]
    psum x1 -> x0, waiting for transfers between devices: 80.7 us -> none  [shards(): sigma = lax.psum(partial_sigma, 'grp')]
    pallas_call x0 -> x1, Pallas kernels: none -> 67.8 us  [shards(): pl.pallas_call(functools.partial(kernel, slices), out_shape=jax.ShapeDtyp...]
    reshape x2 -> x0, local copies, waits for them, and re-layouts: 50.6 us -> none  [the longest x1 25.3 us: shards(): select_pairs(arrived[:, 1])]
    gather x6 -> x0, local copies, waits for them, and re-layouts: 35.2 us -> none  [the longest x2 25.5 us: select_pairs(): return jnp.take(gathered, indices, axis=0)]
    dot_general x2 -> x0, matrix products: 33.3 us -> none  [the longest x1 17 us: shards(): jnp.einsum('spq,sqc->spc', incoming, col_pairs, preferred_element_type=jn...]
    select_n x6 -> x0, other arithmetic: 14.8 us -> none  [the longest x3 14.2 us: select_pairs(): return jnp.take(gathered, indices, axis=0)]
    all_to_all x2 -> x0, starting transfers between devices: 9.52 us -> none  [the longest x1 4.97 us: shards(): lax.all_to_all(outgoing.reshape(regions, CAP, grid_points, grid_points),...]
  transfers between devices with their start and end apart: 4 -> 0, of which waited for: 2 -> 0; matrix products, arithmetic and copies ran while one was open for 21% -> 0% of each run, Pallas kernels for 0% -> 0%
where the time goes in v2:
time: 69.4 us; the launch traced here: 69.3 us
  Pallas kernels  67.8 us (98%)
  local copies, waits for them, and re-layouts  1.47 us (2%)
    pallas_call x1, Pallas kernels, shards(): pl.pallas_call(functools.partial(kernel, slices), out_shape=jax.ShapeDtyp...  67.8 us
    unnamed x1, local copies, waits for them, and re-layouts  1.47 us

profile of v2, /device:TPU:0, one launch (start us, length us, event | category | flops | bytes accessed | tf_op | source)
XLA Modules:
  0.0 69.3 jit_solution(13591938542041455266)
XLA Ops:
  0.0 67.8 %shard_map.73 = f32[1,128,128]{2,1,0:T(8,128)} custom-call(bf16[1,1,512,1024]{3,2,1,0:T(8,128)(2,1)} %orb_hbm.1, bf16[1,1,8,512]{3,2,1,0:T(8,128)(2,1)} %occ_hbm.1, s32[1,128]{1,0:T(1,128)} %bitcast.2, bf16[7,512,512]{2,1,0:T(8,128)(2,1)} %w_hbm.1, s32[7]{0:T(128)} %bitcast.3, s32[7]{0:T(128)} %row_hbm.1, s32[7]{0:T(128)} %col_hbm.1), custom_call_target="tpu_custom_call" | custom-call | tf_op jit(solution)/shard_map/pallas_call | solution.py:321
  67.8 1.5 %copy.9 = f32[1,128,128]{2,1,0:T(8,128)} copy(f32[1,128,128]{2,1,0:T(8,128)} %shard_map.73) | data formatting | bytes 131072

commit v3 on v2

v3 whole, which is shorter than its diff:
```python
import functools

import jax
import jax.numpy as jnp
from jax import lax
from jax.experimental import pallas as pl
from jax.experimental.pallas import tpu as pltpu
from jax.sharding import PartitionSpec as P

MESH = pl.DeviceIdType.MESH
SIDE = 4
STEPS = (1, -1, 2)
COPIES = 256
SPLITS = (
    ("x", 0, "y", "z"),
    ("x", 1, "z", "y"),
    ("y", 0, "z", "x"),
    ("y", 1, "x", "z"),
    ("z", 0, "x", "y"),
    ("z", 1, "y", "x"),
)
HALF = SIDE * SIDE * 2


def mod4(v):
    return lax.rem(v + 2 * SIDE, SIDE)


def kernel(
    slices,
    orb_hbm,
    occ_hbm,
    pidx_hbm,
    w_hbm,
    region_hbm,
    row_hbm,
    col_hbm,
    out_ref,
    *scratch,
):
    count = len(SPLITS)
    bufs, packs, gots = scratch[:count], scratch[count : 2 * count], scratch[2 * count : 3 * count]
    (oc, orb, pidx, wv, wg, acc, part, red, pieces, info, infos) = scratch[3 * count : 3 * count + 11]
    (region, row, col, infos_s, mine_at, pack_at) = scratch[3 * count + 11 : 3 * count + 17]
    local_sem, info_sem, send_sem, recv_sem = scratch[3 * count + 17 :]
    held = w_hbm.shape[0]
    grp = lax.axis_index("grp")
    reg = lax.axis_index("reg")
    me = {"z": grp // SIDE, "x": lax.rem(grp, SIDE), "y": reg // 2}
    core = lax.rem(reg, 2)

    def device(z, x, y, c):
        return (mod4(z) * SIDE + mod4(x), mod4(y) * 2 + c)

    def near(axis, step):
        at = {k: me[k] + (step if k == axis else 0) for k in me}
        return device(at["z"], at["x"], at["y"], core)

    sibling = (grp, me["y"] * 2 + 1 - core)
    sent = []

    def send(src, dst, to):
        n = len(sent)
        copy = pltpu.make_async_remote_copy(
            src, dst, send_sem.at[n], recv_sem.at[n], device_id=to, device_id_type=MESH
        )
        copy.start()
        sent.append(copy)
        return copy

    loads = [
        pltpu.make_async_copy(src, dst, local_sem.at[i])
        for i, (src, dst) in enumerate(
            [
                (pidx_hbm, pidx),
                (orb_hbm.at[0, 0], orb),
                (occ_hbm.at[0, 0], oc.at[0, 0, 0, 0]),
                (region_hbm, region),
                (row_hbm, row),
                (col_hbm, col),
                (w_hbm, wv),
            ]
        )
    ]
    for load in loads[:-1]:
        load.start()
    barrier = pltpu.get_barrier_semaphore()
    partners = [near(axis, step) for axis in "xyz" for step in STEPS] + [sibling]
    for to in partners:
        pl.semaphore_signal(barrier, inc=1, device_id=to, device_id_type=MESH)

    orbs = orb.shape[1]
    width = pidx.shape[1]
    loads[0].wait()
    chosen = (
        lax.broadcasted_iota(jnp.int32, (orbs, width), 0)
        == jnp.broadcast_to(pidx[...], (orbs, width))
    ).astype(jnp.bfloat16)
    loads[1].wait()
    start = 0
    for s, buf in enumerate(bufs):
        buf[0] = jnp.dot(
            orb[start : start + slices[s], :], chosen, preferred_element_type=jnp.float32
        ).astype(jnp.bfloat16)
        start += slices[s]
    for load in loads[2:-1]:
        load.wait()
    sub = lax.broadcasted_iota(jnp.int32, info.shape, 0)
    lane = lax.broadcasted_iota(jnp.int32, info.shape, 1)
    held_info = jnp.zeros(info.shape, jnp.int32)
    for i, ref in enumerate((region, row, col)):
        for n in range(held):
            held_info = jnp.where((sub == i) & (lane == n), ref[n], held_info)
    info[...] = held_info
    pl.semaphore_wait(barrier, len(partners))

    def occ_step(phase):
        even, odd = "xyz"[phase], "zxy"[phase]
        copies = []
        for step in STEPS:
            at = {k: me[k] + step * ((1 - core) * (k == even) + core * (k == odd)) for k in me}
            inner = (0,) * (3 - phase)
            src = oc.at[inner + (0,)]
            dst = oc.at[inner + ((-step) % SIDE,)]
            copies.append(send(src, dst, device(at["z"], at["x"], at["y"], core)))
        return copies

    toward = [(1 - 2 * lax.rem(me[a], 2)) * (1 - 2 * pairing) for a, pairing, _, _ in SPLITS]
    each = range(count)

    def spread(s, t):
        buf, axis = bufs[s], SPLITS[s][2]
        return [send(buf.at[t], buf.at[2 * ((-step) % SIDE) + t], near(axis, step)) for step in STEPS]

    def group(s, low, size):
        buf, axis = bufs[s], SPLITS[s][3]
        return [
            send(
                buf.at[pl.ds(low, size)],
                buf.at[pl.ds(2 * SIDE * ((-step) % SIDE) + low, size)],
                near(axis, step),
            )
            for step in (1, -1)
        ]

    def pass_on(s, side, low, size):
        buf, axis = bufs[s], SPLITS[s][3]
        step = (1, -1)[side]
        low, size = low + side * size // 2, size // 2
        return send(
            buf.at[pl.ds(2 * SIDE * ((-step) % SIDE) + low, size)],
            buf.at[pl.ds(2 * SIDE * 2 + low, size)],
            near(axis, step),
        )

    def mirror(s, c):
        low = 2 * SIDE * c
        return send(
            bufs[s].at[pl.ds(low, 2 * SIDE)], bufs[s].at[pl.ds(HALF + low, 2 * SIDE)], sibling
        )

    def arrive(copies):
        for copy in copies:
            copy.wait_recv()

    swapped = [
        send(bufs[s].at[0], bufs[s].at[1], near(SPLITS[s][0], -toward[s])) for s in each
    ]
    occ_sent = occ_step(0)
    own = [spread(s, 0) for s in each]
    told = [send(info, infos.at[s], near(SPLITS[s][0], toward[s])) for s in each]
    loads[-1].start()

    arrive(occ_sent)
    occ_sent = occ_step(1)
    other, near_groups = [], []
    for s in each:
        swapped[s].wait_recv()
        other.append(spread(s, 1))
        near_groups.append(group(s, 0, 2))
    arrive(occ_sent)
    occ_sent = occ_step(2)

    def distance(d, g):
        parity = lax.rem(d, 2)
        at = {
            "y": mod4(d // 2 - me["y"]),
            "z": mod4(g // SIDE - me["z"]),
            "x": mod4(lax.rem(g, SIDE) - me["x"]),
        }
        return parity, lax.rem(parity + core, 2), at

    def gathered(s, c, at):
        _, _, axis_b, axis_c = SPLITS[s]
        return ((c * SIDE + at[axis_c]) * SIDE + at[axis_b]) * 2

    def find(n, carry):
        for i, ref in enumerate((row, col)):
            _, c, at = distance(region[n], ref[n])
            for s in each:
                along, base = at[SPLITS[s][0]], gathered(s, c, at)
                mine_at[s, 2 * n + i] = jnp.where(
                    along == 0,
                    base,
                    jnp.where(along == 2 + toward[s], base + 1, -1),
                )
        return carry

    lax.fori_loop(0, held, find, 0)

    far_groups, mirrored = [], [[] for s in each]
    for s in each:
        arrive(own[s])
        arrive(other[s])
        far_groups.append(group(s, 2, 2 * SIDE - 2))
        mirrored[s].append(mirror(s, 0))
    passed = [[] for s in each]
    for s in each:
        for side in (0, 1):
            near_groups[s][side].wait_recv()
            passed[s].append(pass_on(s, side, 0, 2))

    arrive(told)
    info_loads = [
        pltpu.make_async_copy(infos.at[s], infos_s.at[s], info_sem.at[s]) for s in each
    ]
    for load in info_loads:
        load.start()
    for load in info_loads:
        load.wait()

    def plan(n, carry):
        for s in each:
            for i in range(2):
                _, c, at = distance(infos_s[s, 0, n], infos_s[s, 1 + i, n])
                base = gathered(s, c, at)
                pack_at[s, 2 * n + i] = jnp.where(at[SPLITS[s][0]] == 0, base, base + 1)
        return carry

    lax.fori_loop(0, held, plan, 0)
    arrive(occ_sent)
    occ_side = send(oc.at[0], oc.at[1], sibling)

    for s in each:
        for side, slot in ((0, 3), (1, 1)):
            far_groups[s][side].wait_recv()
            passed[s].append(pass_on(s, side, 2, 2 * SIDE - 2))
            mirrored[s].append(mirror(s, slot))
    for s in each:
        arrive(passed[s])
        mirrored[s].append(mirror(s, 2))
    fetched = []
    for s in each:
        arrive(mirrored[s])
        for i in range(2 * held):
            packs[s][i] = bufs[s][pack_at[s, i]]
        fetched.append(
            send(
                packs[s],
                gots[s],
                near(SPLITS[s][0], toward[s]),
            )
        )

    occ_side.wait_recv()
    loads[-1].wait()

    def occ_of(n, ref):
        parity, c, at = distance(region[n], ref[n])
        x, y, z = at["x"], at["y"], at["z"]
        return oc[c, z + parity * (y - z), y + parity * (x - y), x + parity * (z - x)]

    def weigh(n, carry):
        gram = lax.dot_general(
            occ_of(n, row),
            occ_of(n, col),
            (((0,), (0,)), ((), ())),
            preferred_element_type=jnp.float32,
        )
        wg[n] = (gram * wv[n].astype(jnp.float32)).astype(jnp.bfloat16)
        return carry

    lax.fori_loop(0, held, weigh, 0)
    arrive(fetched)

    acc[...] = jnp.zeros_like(acc)

    def whole(n, i):
        parts = []
        for s in each:
            at = mine_at[s, 2 * n + i]
            parts.append(jnp.where(at >= 0, bufs[s][jnp.maximum(at, 0)], gots[s][2 * n + i]))
        return jnp.concatenate(parts, axis=0)

    def contract(n, carry):
        screened = jnp.dot(
            wg[n], whole(n, 1), preferred_element_type=jnp.float32
        ).astype(jnp.bfloat16)
        term = lax.dot_general(
            whole(n, 0), screened, (((0,), (0,)), ((), ())), preferred_element_type=jnp.float32
        )
        for c in range(2):
            for y in range(SIDE):
                hit = region[n] == 2 * mod4(me["y"] + y) + lax.rem(core + c, 2)
                acc[c, y] += jnp.where(hit, term, 0.0)
        return carry

    for n in range(held):
        contract(n, 0)

    swaps = {y: send(acc.at[1, y], part.at[y], sibling) for y in (2, 1, 3, 0)}
    far = lambda k: -sum(min(v, SIDE - v) for v in (k // 16, (k // 4) % 4, k % 4))
    rows = pieces.shape[1]
    sums = []
    for y in swaps:
        swaps[y].wait_recv()
        red[y] = acc[0, y] + part[y]
        for k in sorted(range(y, 64, 4), key=far):
            if k:
                z, x = mod4(me["z"] + k // 16), mod4(me["x"] + (k // 4) % 4)
                piece = red.at[y, pl.ds(pl.multiple_of((z * SIDE + x) * rows, rows), rows)]
                sums.append(send(piece, pieces.at[k], device(z, x, me["y"] + y, core)))
    mine = pl.ds(pl.multiple_of(grp * rows, rows), rows)
    total = red[0, mine]
    arrive(sums)
    for k in range(1, 64):
        total = total + pieces[k]
    out_ref[0, mine] = total
    done = [
        send(
            out_ref.at[0, mine],
            out_ref.at[0, mine],
            device(me["z"] + k // 4, me["x"] + k % 4, me["y"], core),
        )
        for k in sorted(range(1, 16), key=far)
    ]
    arrive(done)
    for copy in sent:
        copy.wait_send()


def shards(orbitals, occupied, panel_index, screening, block_region, block_row, block_col):
    held, points = screening.shape[0], screening.shape[1]
    orbs = orbitals.shape[3]
    width = panel_index.shape[0]
    tiles, count = points // 16, len(SPLITS)
    cuts = [(tiles * s + count - 1) // count for s in range(count + 1)]
    slices = [16 * (cuts[s + 1] - cuts[s]) for s in range(count)]
    occ_count = occupied.shape[2]
    hbm = pl.BlockSpec(memory_space=pl.ANY)
    dma = pltpu.SemaphoreType.DMA
    return pl.pallas_call(
        functools.partial(kernel, slices),
        out_shape=jax.ShapeDtypeStruct((1, width, width), jnp.float32),
        in_specs=[hbm] * 7,
        out_specs=pl.BlockSpec(memory_space=pltpu.VMEM),
        scratch_shapes=[
            pltpu.VMEM((2 * HALF, rows, width), jnp.bfloat16) for rows in slices
        ]
        + [pltpu.VMEM((2 * held, rows, width), jnp.bfloat16) for rows in slices] * 2
        + [
            pltpu.VMEM((2, SIDE, SIDE, SIDE, occ_count, points), jnp.bfloat16),
            pltpu.VMEM((points, orbs), jnp.bfloat16),
            pltpu.VMEM((1, width), jnp.int32),
            pltpu.VMEM((held, points, points), jnp.bfloat16),
            pltpu.VMEM((held, points, points), jnp.bfloat16),
            pltpu.VMEM((2, SIDE, width, width), jnp.float32),
            pltpu.VMEM((SIDE, width, width), jnp.float32),
            pltpu.VMEM((SIDE, width, width), jnp.float32),
            pltpu.VMEM((64, width // 16, width), jnp.float32),
            pltpu.VMEM((8, 128), jnp.int32),
            pltpu.VMEM((count, 8, 128), jnp.int32),
            pltpu.SMEM((held,), jnp.int32),
            pltpu.SMEM((held,), jnp.int32),
            pltpu.SMEM((held,), jnp.int32),
            pltpu.SMEM((count, 8, 128), jnp.int32),
            pltpu.SMEM((count, 2 * held), jnp.int32),
            pltpu.SMEM((count, 2 * held), jnp.int32),
            dma((7,)),
            dma((count,)),
            dma((COPIES,)),
            dma((COPIES,)),
        ],
        compiler_params=pltpu.CompilerParams(
            collective_id=0, has_side_effects=True, vmem_limit_bytes=56 * 2**20
        ),
    )(
        orbitals,
        occupied,
        panel_index.reshape(1, width),
        screening,
        block_region.reshape(held),
        block_row,
        block_col,
    )


def solution(mesh):
    in_specs = (
        P("reg", "grp", None, None),
        P("reg", "grp", None, None),
        P(),
        P(("grp", "reg"), None, None),
        P(("grp", "reg"), None),
        P(("grp", "reg")),
        P(("grp", "reg")),
    )
    out_specs = P("reg", None, None)
    return jax.shard_map(shards, mesh=mesh, in_specs=in_specs, out_specs=out_specs, check_vma=False)
```

time: 69.4 us -> 63.9 us (0.921)
  Pallas kernels: 67.8 us -> 62.1 us
    pallas_call x1, Pallas kernels: 67.8 us -> 62.1 us  [shards(): pl.pallas_call(functools.partial(kernel, slices), out_shape=jax.ShapeDtyp...]
where the time goes in v3:
time: 63.9 us; the launch traced here: 63.6 us
  Pallas kernels  62.1 us (97%)
  local copies, waits for them, and re-layouts  1.47 us (2%)
    pallas_call x1, Pallas kernels, shards(): pl.pallas_call(functools.partial(kernel, slices), out_shape=jax.ShapeDtyp...  62.1 us
    unnamed x1, local copies, waits for them, and re-layouts  1.47 us

profile of v3, /device:TPU:0, one launch (start us, length us, event | category | flops | bytes accessed | tf_op | source)
XLA Modules:
  0.0 63.6 jit_solution(9569805816847813054)
XLA Ops:
  0.0 62.1 %shard_map.73 = f32[1,128,128]{2,1,0:T(8,128)} custom-call(bf16[1,1,512,1024]{3,2,1,0:T(8,128)(2,1)} %orb_hbm.1, bf16[1,1,8,512]{3,2,1,0:T(8,128)(2,1)} %occ_hbm.1, s32[1,128]{1,0:T(1,128)} %bitcast.2, bf16[7,512,512]{2,1,0:T(8,128)(2,1)} %w_hbm.1, s32[7]{0:T(128)} %bitcast.3, s32[7]{0:T(128)} %row_hbm.1, s32[7]{0:T(128)} %col_hbm.1), custom_call_target="tpu_custom_call" | custom-call | tf_op jit(solution)/shard_map/pallas_call | solution.py:352
  62.1 1.5 %copy.9 = f32[1,128,128]{2,1,0:T(8,128)} copy(f32[1,128,128]{2,1,0:T(8,128)} %shard_map.73) | data formatting | bytes 131072

commit v4 on v3

--- a/solution.py
+++ b/solution.py
@@ -9,16 +9,8 @@
 
 MESH = pl.DeviceIdType.MESH
 SIDE = 4
-STEPS = (1, -1, 2)
 COPIES = 256
-SPLITS = (
-    ("x", 0, "y", "z"),
-    ("x", 1, "z", "y"),
-    ("y", 0, "z", "x"),
-    ("y", 1, "x", "z"),
-    ("z", 0, "x", "y"),
-    ("z", 1, "y", "x"),
-)
+SPLITS = (("x", "y", "z"), ("y", "z", "x"), ("z", "x", "y"))
 HALF = SIDE * SIDE * 2
 
 
@@ -39,10 +31,10 @@
     *scratch,
 ):
     count = len(SPLITS)
-    bufs, packs, gots = scratch[:count], scratch[count : 2 * count], scratch[2 * count : 3 * count]
-    (oc, orb, pidx, wv, wg, acc, part, red, pieces, info, infos) = scratch[3 * count : 3 * count + 11]
-    (region, row, col, infos_s, mine_at, pack_at) = scratch[3 * count + 11 : 3 * count + 17]
-    local_sem, info_sem, send_sem, recv_sem = scratch[3 * count + 17 :]
+    bufs, packs, gots = scratch[:count], scratch[count : 3 * count], scratch[3 * count : 5 * count]
+    (oc, orb, pidx, wv, wg, acc, part, red, pieces, info, infos) = scratch[5 * count : 5 * count + 11]
+    (region, row, col, infos_s, mine_at, pack_at) = scratch[5 * count + 11 : 5 * count + 17]
+    local_sem, info_sem, send_sem, recv_sem = scratch[5 * count + 17 :]
     held = w_hbm.shape[0]
     grp = lax.axis_index("grp")
     reg = lax.axis_index("reg")
@@ -85,7 +77,7 @@
     for load in loads[:-1]:
         load.start()
     barrier = pltpu.get_barrier_semaphore()
-    partners = [near(axis, step) for axis in "xyz" for step in STEPS] + [sibling]
+    partners = [near(axis, step) for axis in "xyz" for step in (1, -1)] + [sibling]
     for to in partners:
         pl.semaphore_signal(barrier, inc=1, device_id=to, device_id_type=MESH)
 
@@ -114,26 +106,53 @@
     info[...] = held_info
     pl.semaphore_wait(barrier, len(partners))
 
+    def occ_to(phase, step):
+        even, odd = "xyz"[phase], "zxy"[phase]
+        at = {k: me[k] + step * ((1 - core) * (k == even) + core * (k == odd)) for k in me}
+        return device(at["z"], at["x"], at["y"], core)
+
     def occ_step(phase):
-        even, odd = "xyz"[phase], "zxy"[phase]
+        inner = (0,) * (3 - phase)
+        return [
+            send(oc.at[inner + (0,)], oc.at[inner + ((-step) % SIDE,)], occ_to(phase, step))
+            for step in (1, -1)
+        ]
+
+    def occ_pass(phase):
+        inner = (0,) * (3 - phase)
         copies = []
-        for step in STEPS:
-            at = {k: me[k] + step * ((1 - core) * (k == even) + core * (k == odd)) for k in me}
-            inner = (0,) * (3 - phase)
-            src = oc.at[inner + (0,)]
-            dst = oc.at[inner + ((-step) % SIDE,)]
-            copies.append(send(src, dst, device(at["z"], at["x"], at["y"], core)))
+        for side, step in enumerate((1, -1)):
+            if phase == 0 and side == 1:
+                continue
+            half = (pl.ds(2 * side, 2),) if phase else ()
+            src = oc.at[inner + ((-step) % SIDE,) + half]
+            dst = oc.at[inner + (2,) + half]
+            copies.append(send(src, dst, occ_to(phase, step)))
         return copies
 
-    toward = [(1 - 2 * lax.rem(me[a], 2)) * (1 - 2 * pairing) for a, pairing, _, _ in SPLITS]
     each = range(count)
-
-    def spread(s, t):
+    ways = [(s, way) for s in each for way in (0, 1)]
+    toward = [
+        (1 - 2 * lax.rem(me[SPLITS[s][0]], 2)) * (1 - 2 * way) for s, way in ways
+    ]
+    cuts = [16 * ((rows + 31) // 32) for rows in slices]
+    halves = [
+        pl.ds(0, cuts[s]) if way == 0 else pl.ds(cuts[s], slices[s] - cuts[s]) for s, way in ways
+    ]
+
+    def spread(s, t, size, steps):
+        buf, axis = bufs[s], SPLITS[s][1]
+        return [
+            send(
+                buf.at[pl.ds(t, size)],
+                buf.at[pl.ds(2 * ((-step) % SIDE) + t, size)],
+                near(axis, step),
+            )
+            for step in steps
+        ]
+
+    def group(s, low, size):
         buf, axis = bufs[s], SPLITS[s][2]
-        return [send(buf.at[t], buf.at[2 * ((-step) % SIDE) + t], near(axis, step)) for step in STEPS]
-
-    def group(s, low, size):
-        buf, axis = bufs[s], SPLITS[s][3]
         return [
             send(
                 buf.at[pl.ds(low, size)],
@@ -144,7 +163,7 @@
         ]
 
     def pass_on(s, side, low, size):
-        buf, axis = bufs[s], SPLITS[s][3]
+        buf, axis = bufs[s], SPLITS[s][2]
         step = (1, -1)[side]
         low, size = low + side * size // 2, size // 2
         return send(
@@ -164,22 +183,24 @@
             copy.wait_recv()
 
     swapped = [
-        send(bufs[s].at[0], bufs[s].at[1], near(SPLITS[s][0], -toward[s])) for s in each
-    ]
+        send(bufs[s].at[0, halves[w]], bufs[s].at[1, halves[w]], near(SPLITS[s][0], -toward[w]))
+        for w, (s, way) in enumerate(ways)
+    ]
+    own = [spread(s, 0, 1, (1, -1)) for s in each]
     occ_sent = occ_step(0)
-    own = [spread(s, 0) for s in each]
-    told = [send(info, infos.at[s], near(SPLITS[s][0], toward[s])) for s in each]
+    told = [
+        send(info, infos.at[w], near(SPLITS[s][0], toward[w])) for w, (s, way) in enumerate(ways)
+    ]
     loads[-1].start()
 
-    arrive(occ_sent)
-    occ_sent = occ_step(1)
     other, near_groups = [], []
     for s in each:
-        swapped[s].wait_recv()
-        other.append(spread(s, 1))
+        arrive(own[s])
+        arrive(swapped[2 * s : 2 * s + 2])
+        other.append(spread(s, 1, 1, (1, -1)) + spread(s, 0, 2, (2,)))
         near_groups.append(group(s, 0, 2))
     arrive(occ_sent)
-    occ_sent = occ_step(2)
+    occ_sent = occ_pass(0)
 
     def distance(d, g):
         parity = lax.rem(d, 2)
@@ -191,18 +212,18 @@
         return parity, lax.rem(parity + core, 2), at
 
     def gathered(s, c, at):
-        _, _, axis_b, axis_c = SPLITS[s]
+        _, axis_b, axis_c = SPLITS[s]
         return ((c * SIDE + at[axis_c]) * SIDE + at[axis_b]) * 2
 
     def find(n, carry):
         for i, ref in enumerate((row, col)):
             _, c, at = distance(region[n], ref[n])
-            for s in each:
+            for w, (s, way) in enumerate(ways):
                 along, base = at[SPLITS[s][0]], gathered(s, c, at)
-                mine_at[s, 2 * n + i] = jnp.where(
+                mine_at[w, 2 * n + i] = jnp.where(
                     along == 0,
                     base,
-                    jnp.where(along == 2 + toward[s], base + 1, -1),
+                    jnp.where(along == 2 + toward[w], base + 1, -1),
                 )
         return carry
 
@@ -210,7 +231,6 @@
 
     far_groups, mirrored = [], [[] for s in each]
     for s in each:
-        arrive(own[s])
         arrive(other[s])
         far_groups.append(group(s, 2, 2 * SIDE - 2))
         mirrored[s].append(mirror(s, 0))
@@ -219,10 +239,12 @@
         for side in (0, 1):
             near_groups[s][side].wait_recv()
             passed[s].append(pass_on(s, side, 0, 2))
+    arrive(occ_sent)
+    occ_sent = occ_step(1)
 
     arrive(told)
     info_loads = [
-        pltpu.make_async_copy(infos.at[s], infos_s.at[s], info_sem.at[s]) for s in each
+        pltpu.make_async_copy(infos.at[w], infos_s.at[w], info_sem.at[w]) for w in range(2 * count)
     ]
     for load in info_loads:
         load.start()
@@ -230,37 +252,38 @@
         load.wait()
 
     def plan(n, carry):
-        for s in each:
+        for w, (s, way) in enumerate(ways):
             for i in range(2):
-                _, c, at = distance(infos_s[s, 0, n], infos_s[s, 1 + i, n])
+                _, c, at = distance(infos_s[w, 0, n], infos_s[w, 1 + i, n])
                 base = gathered(s, c, at)
-                pack_at[s, 2 * n + i] = jnp.where(at[SPLITS[s][0]] == 0, base, base + 1)
+                pack_at[w, 2 * n + i] = jnp.where(at[SPLITS[s][0]] == 0, base, base + 1)
         return carry
 
     lax.fori_loop(0, held, plan, 0)
     arrive(occ_sent)
-    occ_side = send(oc.at[0], oc.at[1], sibling)
+    occ_sent = occ_pass(1)
 
     for s in each:
         for side, slot in ((0, 3), (1, 1)):
             far_groups[s][side].wait_recv()
             passed[s].append(pass_on(s, side, 2, 2 * SIDE - 2))
             mirrored[s].append(mirror(s, slot))
+    arrive(occ_sent)
+    occ_sent = occ_step(2)
     for s in each:
         arrive(passed[s])
         mirrored[s].append(mirror(s, 2))
+    arrive(occ_sent)
+    occ_sent = occ_pass(2)
     fetched = []
-    for s in each:
-        arrive(mirrored[s])
+    for w, (s, way) in enumerate(ways):
+        if way == 0:
+            arrive(mirrored[s])
         for i in range(2 * held):
-            packs[s][i] = bufs[s][pack_at[s, i]]
-        fetched.append(
-            send(
-                packs[s],
-                gots[s],
-                near(SPLITS[s][0], toward[s]),
-            )
-        )
+            packs[w][i] = bufs[s][pack_at[w, i], halves[w]]
+        fetched.append(send(packs[w], gots[w], near(SPLITS[s][0], toward[w])))
+    arrive(occ_sent)
+    occ_side = send(oc.at[0], oc.at[1], sibling)
 
     occ_side.wait_recv()
     loads[-1].wait()
@@ -287,9 +310,10 @@
 
     def whole(n, i):
         parts = []
-        for s in each:
-            at = mine_at[s, 2 * n + i]
-            parts.append(jnp.where(at >= 0, bufs[s][jnp.maximum(at, 0)], gots[s][2 * n + i]))
+        for w, (s, way) in enumerate(ways):
+            at = mine_at[w, 2 * n + i]
+            mine = bufs[s][jnp.maximum(at, 0), halves[w]]
+            parts.append(jnp.where(at >= 0, mine, gots[w][2 * n + i]))
         return jnp.concatenate(parts, axis=0)
 
     def contract(n, carry):
@@ -344,8 +368,11 @@
     orbs = orbitals.shape[3]
     width = panel_index.shape[0]
     tiles, count = points // 16, len(SPLITS)
-    cuts = [(tiles * s + count - 1) // count for s in range(count + 1)]
+    cuts = [0, tiles * 5 // 16, tiles * 11 // 16, tiles]
     slices = [16 * (cuts[s + 1] - cuts[s]) for s in range(count)]
+    halves = []
+    for rows in slices:
+        halves += [16 * ((rows + 31) // 32), rows - 16 * ((rows + 31) // 32)]
     occ_count = occupied.shape[2]
     hbm = pl.BlockSpec(memory_space=pl.ANY)
     dma = pltpu.SemaphoreType.DMA
@@ -357,7 +384,7 @@
         scratch_shapes=[
             pltpu.VMEM((2 * HALF, rows, width), jnp.bfloat16) for rows in slices
         ]
-        + [pltpu.VMEM((2 * held, rows, width), jnp.bfloat16) for rows in slices] * 2
+        + [pltpu.VMEM((2 * held, rows, width), jnp.bfloat16) for rows in halves] * 2
         + [
             pltpu.VMEM((2, SIDE, SIDE, SIDE, occ_count, points), jnp.bfloat16),
             pltpu.VMEM((points, orbs), jnp.bfloat16),
@@ -369,15 +396,15 @@
             pltpu.VMEM((SIDE, width, width), jnp.float32),
             pltpu.VMEM((64, width // 16, width), jnp.float32),
             pltpu.VMEM((8, 128), jnp.int32),
-            pltpu.VMEM((count, 8, 128), jnp.int32),
+            pltpu.VMEM((2 * count, 8, 128), jnp.int32),
             pltpu.SMEM((held,), jnp.int32),
             pltpu.SMEM((held,), jnp.int32),
             pltpu.SMEM((held,), jnp.int32),
-            pltpu.SMEM((count, 8, 128), jnp.int32),
-            pltpu.SMEM((count, 2 * held), jnp.int32),
-            pltpu.SMEM((count, 2 * held), jnp.int32),
+            pltpu.SMEM((2 * count, 8, 128), jnp.int32),
+            pltpu.SMEM((2 * count, 2 * held), jnp.int32),
+            pltpu.SMEM((2 * count, 2 * held), jnp.int32),
             dma((7,)),
-            dma((count,)),
+            dma((2 * count,)),
             dma((COPIES,)),
             dma((COPIES,)),
         ],

time: 63.9 us -> 63.9 us (level)
  no operation moved by 1% of the time
where the time goes in v4:
time: 63.9 us; the launch traced here: 63.7 us
  Pallas kernels  62.2 us (97%)
  local copies, waits for them, and re-layouts  1.47 us (2%)
    pallas_call x1, Pallas kernels, shards(): pl.pallas_call(functools.partial(kernel, slices), out_shape=jax.ShapeDtyp...  62.2 us
    unnamed x1, local copies, waits for them, and re-layouts  1.47 us

profile of v4, /device:TPU:0, one launch (start us, length us, event | category | flops | bytes accessed | tf_op | source)
XLA Modules:
  0.0 63.7 jit_solution(8017952240211291666)
XLA Ops:
  0.0 62.2 %shard_map.73 = f32[1,128,128]{2,1,0:T(8,128)} custom-call(bf16[1,1,512,1024]{3,2,1,0:T(8,128)(2,1)} %orb_hbm.1, bf16[1,1,8,512]{3,2,1,0:T(8,128)(2,1)} %occ_hbm.1, s32[1,128]{1,0:T(1,128)} %bitcast.2, bf16[7,512,512]{2,1,0:T(8,128)(2,1)} %w_hbm.1, s32[7]{0:T(128)} %bitcast.3, s32[7]{0:T(128)} %row_hbm.1, s32[7]{0:T(128)} %col_hbm.1), custom_call_target="tpu_custom_call" | custom-call | tf_op jit(solution)/shard_map/pallas_call | solution.py:379
  62.2 1.5 %copy.9 = f32[1,128,128]{2,1,0:T(8,128)} copy(f32[1,128,128]{2,1,0:T(8,128)} %shard_map.73) | data formatting | bytes 131072

commit v5 on v4

--- a/solution.py
+++ b/solution.py
@@ -11,6 +11,7 @@
 SIDE = 4
 COPIES = 256
 SPLITS = (("x", "y", "z"), ("y", "z", "x"), ("z", "x", "y"))
+PLACE = {1: 2, -1: 1, 2: 3}
 HALF = SIDE * SIDE * 2
 
 
@@ -111,41 +112,28 @@
         at = {k: me[k] + step * ((1 - core) * (k == even) + core * (k == odd)) for k in me}
         return device(at["z"], at["x"], at["y"], core)
 
-    def occ_step(phase):
+    def occ_step(phase, steps):
         inner = (0,) * (3 - phase)
         return [
             send(oc.at[inner + (0,)], oc.at[inner + ((-step) % SIDE,)], occ_to(phase, step))
-            for step in (1, -1)
+            for step in steps
         ]
-
-    def occ_pass(phase):
-        inner = (0,) * (3 - phase)
-        copies = []
-        for side, step in enumerate((1, -1)):
-            if phase == 0 and side == 1:
-                continue
-            half = (pl.ds(2 * side, 2),) if phase else ()
-            src = oc.at[inner + ((-step) % SIDE,) + half]
-            dst = oc.at[inner + (2,) + half]
-            copies.append(send(src, dst, occ_to(phase, step)))
-        return copies
 
     each = range(count)
     ways = [(s, way) for s in each for way in (0, 1)]
-    toward = [
-        (1 - 2 * lax.rem(me[SPLITS[s][0]], 2)) * (1 - 2 * way) for s, way in ways
-    ]
+    toward = [(1 - 2 * lax.rem(me[SPLITS[s][0]], 2)) * (1 - 2 * way) for s, way in ways]
     cuts = [16 * ((rows + 31) // 32) for rows in slices]
     halves = [
         pl.ds(0, cuts[s]) if way == 0 else pl.ds(cuts[s], slices[s] - cuts[s]) for s, way in ways
     ]
+    unit = 2 * SIDE
 
     def spread(s, t, size, steps):
         buf, axis = bufs[s], SPLITS[s][1]
         return [
             send(
                 buf.at[pl.ds(t, size)],
-                buf.at[pl.ds(2 * ((-step) % SIDE) + t, size)],
+                buf.at[pl.ds(2 * PLACE[step] + t, size)],
                 near(axis, step),
             )
             for step in steps
@@ -156,7 +144,7 @@
         return [
             send(
                 buf.at[pl.ds(low, size)],
-                buf.at[pl.ds(2 * SIDE * ((-step) % SIDE) + low, size)],
+                buf.at[pl.ds(unit * PLACE[step] + low, size)],
                 near(axis, step),
             )
             for step in (1, -1)
@@ -167,40 +155,25 @@
         step = (1, -1)[side]
         low, size = low + side * size // 2, size // 2
         return send(
-            buf.at[pl.ds(2 * SIDE * ((-step) % SIDE) + low, size)],
-            buf.at[pl.ds(2 * SIDE * 2 + low, size)],
+            buf.at[pl.ds(unit * PLACE[step] + low, size)],
+            buf.at[pl.ds(unit * PLACE[2] + low, size)],
             near(axis, step),
         )
 
-    def mirror(s, c):
-        low = 2 * SIDE * c
-        return send(
-            bufs[s].at[pl.ds(low, 2 * SIDE)], bufs[s].at[pl.ds(HALF + low, 2 * SIDE)], sibling
-        )
+    def mirror(s, low, size):
+        buf = bufs[s]
+        return send(buf.at[pl.ds(low, size)], buf.at[pl.ds(HALF + low, size)], sibling)
 
     def arrive(copies):
         for copy in copies:
             copy.wait_recv()
 
-    swapped = [
-        send(bufs[s].at[0, halves[w]], bufs[s].at[1, halves[w]], near(SPLITS[s][0], -toward[w]))
-        for w, (s, way) in enumerate(ways)
-    ]
-    own = [spread(s, 0, 1, (1, -1)) for s in each]
-    occ_sent = occ_step(0)
-    told = [
-        send(info, infos.at[w], near(SPLITS[s][0], toward[w])) for w, (s, way) in enumerate(ways)
-    ]
-    loads[-1].start()
-
-    other, near_groups = [], []
-    for s in each:
-        arrive(own[s])
-        arrive(swapped[2 * s : 2 * s + 2])
-        other.append(spread(s, 1, 1, (1, -1)) + spread(s, 0, 2, (2,)))
-        near_groups.append(group(s, 0, 2))
-    arrive(occ_sent)
-    occ_sent = occ_pass(0)
+    passed, mirrored = [[] for s in each], [[] for s in each]
+
+    def relay(s, copies, low, size):
+        for side in (0, 1):
+            copies[side].wait_recv()
+            passed[s].append(pass_on(s, side, low, size))
 
     def distance(d, g):
         parity = lax.rem(d, 2)
@@ -213,7 +186,8 @@
 
     def gathered(s, c, at):
         _, axis_b, axis_c = SPLITS[s]
-        return ((c * SIDE + at[axis_c]) * SIDE + at[axis_b]) * 2
+        b_at, c_at = (at[k] + (at[k] // 2) * (5 - 2 * at[k]) for k in (axis_b, axis_c))
+        return ((c * SIDE + c_at) * SIDE + b_at) * 2
 
     def find(n, carry):
         for i, ref in enumerate((row, col)):
@@ -221,35 +195,9 @@
             for w, (s, way) in enumerate(ways):
                 along, base = at[SPLITS[s][0]], gathered(s, c, at)
                 mine_at[w, 2 * n + i] = jnp.where(
-                    along == 0,
-                    base,
-                    jnp.where(along == 2 + toward[w], base + 1, -1),
+                    along == 0, base, jnp.where(along == 2 + toward[w], base + 1, -1)
                 )
         return carry
-
-    lax.fori_loop(0, held, find, 0)
-
-    far_groups, mirrored = [], [[] for s in each]
-    for s in each:
-        arrive(other[s])
-        far_groups.append(group(s, 2, 2 * SIDE - 2))
-        mirrored[s].append(mirror(s, 0))
-    passed = [[] for s in each]
-    for s in each:
-        for side in (0, 1):
-            near_groups[s][side].wait_recv()
-            passed[s].append(pass_on(s, side, 0, 2))
-    arrive(occ_sent)
-    occ_sent = occ_step(1)
-
-    arrive(told)
-    info_loads = [
-        pltpu.make_async_copy(infos.at[w], infos_s.at[w], info_sem.at[w]) for w in range(2 * count)
-    ]
-    for load in info_loads:
-        load.start()
-    for load in info_loads:
-        load.wait()
 
     def plan(n, carry):
         for w, (s, way) in enumerate(ways):
@@ -259,22 +207,65 @@
                 pack_at[w, 2 * n + i] = jnp.where(at[SPLITS[s][0]] == 0, base, base + 1)
         return carry
 
+    swapped = [
+        send(bufs[s].at[0, halves[w]], bufs[s].at[1, halves[w]], near(SPLITS[s][0], -toward[w]))
+        for w, (s, way) in enumerate(ways)
+    ]
+    own = [spread(s, 0, 1, (1, -1)) for s in each]
+    occ_sent = occ_step(0, (1, -1))
+    straight = [group(s, 0, 1) for s in each]
+    told = [
+        send(info, infos.at[w], near(SPLITS[s][0], toward[w])) for w, (s, way) in enumerate(ways)
+    ]
+    loads[-1].start()
+
+    other = []
+    for s in each:
+        arrive(own[s])
+        own_far = spread(s, 0, 1, (2,))
+        arrive(swapped[2 * s : 2 * s + 2])
+        other.append(spread(s, 1, 1, (1, -1, 2)) + own_far)
+    crossed = [group(s, 1, 1) for s in each]
+    arrive(occ_sent)
+    occ_sent = occ_step(0, (2,))
+    lax.fori_loop(0, held, find, 0)
+
+    near_groups, far_groups = [], []
+    for s in each:
+        arrive(other[s][:2])
+        near_groups.append(group(s, 2, 4))
+    arrive(occ_sent)
+    occ_sent = occ_step(1, (1, -1, 2))
+    for s in each:
+        arrive(other[s][2:])
+        far_groups.append(group(s, 6, 2))
+        mirrored[s].append(mirror(s, 0, unit))
+    for s in each:
+        relay(s, (straight[s][0], crossed[s][1]), 0, 2)
+
+    arrive(told)
+    info_loads = [
+        pltpu.make_async_copy(infos.at[w], infos_s.at[w], info_sem.at[w]) for w in range(2 * count)
+    ]
+    for load in info_loads:
+        load.start()
+    for load in info_loads:
+        load.wait()
     lax.fori_loop(0, held, plan, 0)
     arrive(occ_sent)
-    occ_sent = occ_pass(1)
-
-    for s in each:
-        for side, slot in ((0, 3), (1, 1)):
-            far_groups[s][side].wait_recv()
-            passed[s].append(pass_on(s, side, 2, 2 * SIDE - 2))
-            mirrored[s].append(mirror(s, slot))
+    occ_sent = occ_step(2, (1, -1, 2))
+
+    for s in each:
+        relay(s, near_groups[s], 2, 4)
+    for s in each:
+        relay(s, far_groups[s], 6, 2)
+        arrive((straight[s][1], crossed[s][0]))
+        mirrored[s].append(mirror(s, unit, 2 * unit))
+    for s in each:
+        arrive(passed[s])
+        mirrored[s].append(mirror(s, 3 * unit, unit))
     arrive(occ_sent)
-    occ_sent = occ_step(2)
-    for s in each:
-        arrive(passed[s])
-        mirrored[s].append(mirror(s, 2))
-    arrive(occ_sent)
-    occ_sent = occ_pass(2)
+    occ_side = send(oc.at[0], oc.at[1], sibling)
     fetched = []
     for w, (s, way) in enumerate(ways):
         if way == 0:
@@ -282,8 +273,6 @@
         for i in range(2 * held):
             packs[w][i] = bufs[s][pack_at[w, i], halves[w]]
         fetched.append(send(packs[w], gots[w], near(SPLITS[s][0], toward[w])))
-    arrive(occ_sent)
-    occ_side = send(oc.at[0], oc.at[1], sibling)
 
     occ_side.wait_recv()
     loads[-1].wait()
@@ -317,12 +306,10 @@
         return jnp.concatenate(parts, axis=0)
 
     def contract(n, carry):
-        screened = jnp.dot(
-            wg[n], whole(n, 1), preferred_element_type=jnp.float32
+        turned = lax.dot_general(
+            whole(n, 0), wg[n], (((0,), (0,)), ((), ())), preferred_element_type=jnp.float32
         ).astype(jnp.bfloat16)
-        term = lax.dot_general(
-            whole(n, 0), screened, (((0,), (0,)), ((), ())), preferred_element_type=jnp.float32
-        )
+        term = jnp.dot(turned, whole(n, 1), preferred_element_type=jnp.float32)
         for c in range(2):
             for y in range(SIDE):
                 hit = region[n] == 2 * mod4(me["y"] + y) + lax.rem(core + c, 2)
@@ -349,16 +336,19 @@
     arrive(sums)
     for k in range(1, 64):
         total = total + pieces[k]
-    out_ref[0, mine] = total
+    pieces[0] = total
+    keep = pltpu.make_async_copy(pieces.at[0], out_ref.at[0, mine], info_sem.at[0])
+    keep.start()
     done = [
         send(
-            out_ref.at[0, mine],
+            pieces.at[0],
             out_ref.at[0, mine],
             device(me["z"] + k // 4, me["x"] + k % 4, me["y"], core),
         )
         for k in sorted(range(1, 16), key=far)
     ]
     arrive(done)
+    keep.wait()
     for copy in sent:
         copy.wait_send()
 
@@ -368,7 +358,7 @@
     orbs = orbitals.shape[3]
     width = panel_index.shape[0]
     tiles, count = points // 16, len(SPLITS)
-    cuts = [0, tiles * 5 // 16, tiles * 11 // 16, tiles]
+    cuts = [0, tiles * 11 // 32, tiles * 11 // 16, tiles]
     slices = [16 * (cuts[s + 1] - cuts[s]) for s in range(count)]
     halves = []
     for rows in slices:
@@ -380,7 +370,7 @@
         functools.partial(kernel, slices),
         out_shape=jax.ShapeDtypeStruct((1, width, width), jnp.float32),
         in_specs=[hbm] * 7,
-        out_specs=pl.BlockSpec(memory_space=pltpu.VMEM),
+        out_specs=pl.BlockSpec(memory_space=pl.ANY),
         scratch_shapes=[
             pltpu.VMEM((2 * HALF, rows, width), jnp.bfloat16) for rows in slices
         ]

time: 63.9 us -> 59.7 us (0.934)
  Pallas kernels: 62.2 us -> 58 us
    pallas_call x1, Pallas kernels: 62.2 us -> 58 us  [shards(): pl.pallas_call(functools.partial(kernel, slices), out_shape=jax.ShapeDtyp...]
where the time goes in v5:
time: 59.7 us; the launch traced here: 59.5 us
  Pallas kernels  58 us (97%)
  local copies, waits for them, and re-layouts  1.47 us (2%)
    pallas_call x1, Pallas kernels, shards(): pl.pallas_call(functools.partial(kernel, slices), out_shape=jax.ShapeDtyp...  58 us
    unnamed x1, local copies, waits for them, and re-layouts  1.47 us

profile of v5, /device:TPU:0, one launch (start us, length us, event | category | flops | bytes accessed | tf_op | source)
XLA Modules:
  0.0 59.5 jit_solution(9662508181021085579)
XLA Ops:
  0.0 58.0 %shard_map.73 = f32[1,128,128]{2,1,0:T(8,128)} custom-call(bf16[1,1,512,1024]{3,2,1,0:T(8,128)(2,1)} %orb_hbm.1, bf16[1,1,8,512]{3,2,1,0:T(8,128)(2,1)} %occ_hbm.1, s32[1,128]{1,0:T(1,128)} %bitcast.2, bf16[7,512,512]{2,1,0:T(8,128)(2,1)} %w_hbm.1, s32[7]{0:T(128)} %bitcast.3, s32[7]{0:T(128)} %row_hbm.1, s32[7]{0:T(128)} %col_hbm.1), custom_call_target="tpu_custom_call" | custom-call | tf_op jit(solution)/shard_map/pallas_call | solution.py:369
  58.0 1.5 %copy.9 = f32[1,128,128]{2,1,0:T(8,128)} copy(f32[1,128,128]{2,1,0:T(8,128)} %shard_map.73) | data formatting | bytes 131072

commit v6 on v5

--- a/solution.py
+++ b/solution.py
@@ -305,19 +305,18 @@
             parts.append(jnp.where(at >= 0, mine, gots[w][2 * n + i]))
         return jnp.concatenate(parts, axis=0)
 
-    def contract(n, carry):
-        turned = lax.dot_general(
+    turned = [
+        lax.dot_general(
             whole(n, 0), wg[n], (((0,), (0,)), ((), ())), preferred_element_type=jnp.float32
         ).astype(jnp.bfloat16)
-        term = jnp.dot(turned, whole(n, 1), preferred_element_type=jnp.float32)
+        for n in range(held)
+    ]
+    for n in range(held):
+        term = jnp.dot(turned[n], whole(n, 1), preferred_element_type=jnp.float32)
         for c in range(2):
             for y in range(SIDE):
                 hit = region[n] == 2 * mod4(me["y"] + y) + lax.rem(core + c, 2)
                 acc[c, y] += jnp.where(hit, term, 0.0)
-        return carry
-
-    for n in range(held):
-        contract(n, 0)
 
     swaps = {y: send(acc.at[1, y], part.at[y], sibling) for y in (2, 1, 3, 0)}
     far = lambda k: -sum(min(v, SIDE - v) for v in (k // 16, (k // 4) % 4, k % 4))

time: 59.7 us -> 59.2 us (level)
  no operation moved by 1% of the time
where the time goes in v6:
time: 59.2 us; the launch traced here: 59 us
  Pallas kernels  57.5 us (97%)
  local copies, waits for them, and re-layouts  1.47 us (2%)
    pallas_call x1, Pallas kernels, shards(): pl.pallas_call(functools.partial(kernel, slices), out_shape=jax.ShapeDtyp...  57.5 us
    unnamed x1, local copies, waits for them, and re-layouts  1.47 us

profile of v6, /device:TPU:0, one launch (start us, length us, event | category | flops | bytes accessed | tf_op | source)
XLA Modules:
  0.0 59.0 jit_solution(6761957509575785131)
XLA Ops:
  0.0 57.5 %shard_map.73 = f32[1,128,128]{2,1,0:T(8,128)} custom-call(bf16[1,1,512,1024]{3,2,1,0:T(8,128)(2,1)} %orb_hbm.1, bf16[1,1,8,512]{3,2,1,0:T(8,128)(2,1)} %occ_hbm.1, s32[1,128]{1,0:T(1,128)} %bitcast.2, bf16[7,512,512]{2,1,0:T(8,128)(2,1)} %w_hbm.1, s32[7]{0:T(128)} %bitcast.3, s32[7]{0:T(128)} %row_hbm.1, s32[7]{0:T(128)} %col_hbm.1), custom_call_target="tpu_custom_call" | custom-call | tf_op jit(solution)/shard_map/pallas_call | solution.py:368
  57.5 1.5 %copy.9 = f32[1,128,128]{2,1,0:T(8,128)} copy(f32[1,128,128]{2,1,0:T(8,128)} %shard_map.73) | data formatting | bytes 131072

commit v7 on v6

--- a/solution.py
+++ b/solution.py
@@ -207,16 +207,13 @@
                 pack_at[w, 2 * n + i] = jnp.where(at[SPLITS[s][0]] == 0, base, base + 1)
         return carry
 
+    own = [spread(s, 0, 1, (1, -1)) for s in each]
     swapped = [
         send(bufs[s].at[0, halves[w]], bufs[s].at[1, halves[w]], near(SPLITS[s][0], -toward[w]))
         for w, (s, way) in enumerate(ways)
     ]
-    own = [spread(s, 0, 1, (1, -1)) for s in each]
     occ_sent = occ_step(0, (1, -1))
     straight = [group(s, 0, 1) for s in each]
-    told = [
-        send(info, infos.at[w], near(SPLITS[s][0], toward[w])) for w, (s, way) in enumerate(ways)
-    ]
     loads[-1].start()
 
     other = []
@@ -228,6 +225,9 @@
     crossed = [group(s, 1, 1) for s in each]
     arrive(occ_sent)
     occ_sent = occ_step(0, (2,))
+    told = [
+        send(info, infos.at[w], near(SPLITS[s][0], toward[w])) for w, (s, way) in enumerate(ways)
+    ]
     lax.fori_loop(0, held, find, 0)
 
     near_groups, far_groups = [], []
@@ -262,8 +262,11 @@
         arrive((straight[s][1], crossed[s][0]))
         mirrored[s].append(mirror(s, unit, 2 * unit))
     for s in each:
-        arrive(passed[s])
-        mirrored[s].append(mirror(s, 3 * unit, unit))
+        arrive(passed[s][:4])
+        mirrored[s].append(mirror(s, 3 * unit, 6))
+    for s in each:
+        arrive(passed[s][4:])
+        mirrored[s].append(mirror(s, 3 * unit + 6, 2))
     arrive(occ_sent)
     occ_side = send(oc.at[0], oc.at[1], sibling)
     fetched = []

time: 59.2 us -> 58.6 us (0.990)
  no operation moved by 1% of the time
where the time goes in v7:
time: 58.6 us; the launch traced here: 58.4 us
  Pallas kernels  57 us (97%)
  local copies, waits for them, and re-layouts  1.47 us (3%)
    pallas_call x1, Pallas kernels, shards(): pl.pallas_call(functools.partial(kernel, slices), out_shape=jax.ShapeDtyp...  57 us
    unnamed x1, local copies, waits for them, and re-layouts  1.47 us

profile of v7, /device:TPU:0, one launch (start us, length us, event | category | flops | bytes accessed | tf_op | source)
XLA Modules:
  0.0 58.4 jit_solution(1199828860439508089)
XLA Ops:
  0.0 57.0 %shard_map.73 = f32[1,128,128]{2,1,0:T(8,128)} custom-call(bf16[1,1,512,1024]{3,2,1,0:T(8,128)(2,1)} %orb_hbm.1, bf16[1,1,8,512]{3,2,1,0:T(8,128)(2,1)} %occ_hbm.1, s32[1,128]{1,0:T(1,128)} %bitcast.2, bf16[7,512,512]{2,1,0:T(8,128)(2,1)} %w_hbm.1, s32[7]{0:T(128)} %bitcast.3, s32[7]{0:T(128)} %row_hbm.1, s32[7]{0:T(128)} %col_hbm.1), custom_call_target="tpu_custom_call" | custom-call | tf_op jit(solution)/shard_map/pallas_call | solution.py:371
  57.0 1.5 %copy.9 = f32[1,128,128]{2,1,0:T(8,128)} copy(f32[1,128,128]{2,1,0:T(8,128)} %shard_map.73) | data formatting | bytes 131072

commit v8 on v7

--- a/solution.py
+++ b/solution.py
@@ -194,7 +194,7 @@
             _, c, at = distance(region[n], ref[n])
             for w, (s, way) in enumerate(ways):
                 along, base = at[SPLITS[s][0]], gathered(s, c, at)
-                mine_at[w, 2 * n + i] = jnp.where(
+                mine_at[w, held * i + n] = jnp.where(
                     along == 0, base, jnp.where(along == 2 + toward[w], base + 1, -1)
                 )
         return carry
@@ -204,7 +204,7 @@
             for i in range(2):
                 _, c, at = distance(infos_s[w, 0, n], infos_s[w, 1 + i, n])
                 base = gathered(s, c, at)
-                pack_at[w, 2 * n + i] = jnp.where(at[SPLITS[s][0]] == 0, base, base + 1)
+                pack_at[w, held * i + n] = jnp.where(at[SPLITS[s][0]] == 0, base, base + 1)
         return carry
 
     own = [spread(s, 0, 1, (1, -1)) for s in each]
@@ -269,13 +269,16 @@
         mirrored[s].append(mirror(s, 3 * unit + 6, 2))
     arrive(occ_sent)
     occ_side = send(oc.at[0], oc.at[1], sibling)
-    fetched = []
-    for w, (s, way) in enumerate(ways):
-        if way == 0:
-            arrive(mirrored[s])
-        for i in range(2 * held):
-            packs[w][i] = bufs[s][pack_at[w, i], halves[w]]
-        fetched.append(send(packs[w], gots[w], near(SPLITS[s][0], toward[w])))
+    fetched = [[], []]
+    for i in range(2):
+        part_of = pl.ds(held * i, held)
+        for w, (s, way) in enumerate(ways):
+            if i == 0 and way == 0:
+                arrive(mirrored[s])
+            for n in range(held * i, held * i + held):
+                packs[w][n] = bufs[s][pack_at[w, n], halves[w]]
+            to = near(SPLITS[s][0], toward[w])
+            fetched[i].append(send(packs[w].at[part_of], gots[w].at[part_of], to))
 
     occ_side.wait_recv()
     loads[-1].wait()
@@ -296,16 +299,16 @@
         return carry
 
     lax.fori_loop(0, held, weigh, 0)
-    arrive(fetched)
+    arrive(fetched[0])
 
     acc[...] = jnp.zeros_like(acc)
 
     def whole(n, i):
         parts = []
         for w, (s, way) in enumerate(ways):
-            at = mine_at[w, 2 * n + i]
+            at = mine_at[w, held * i + n]
             mine = bufs[s][jnp.maximum(at, 0), halves[w]]
-            parts.append(jnp.where(at >= 0, mine, gots[w][2 * n + i]))
+            parts.append(jnp.where(at >= 0, mine, gots[w][held * i + n]))
         return jnp.concatenate(parts, axis=0)
 
     turned = [
@@ -314,6 +317,7 @@
         ).astype(jnp.bfloat16)
         for n in range(held)
     ]
+    arrive(fetched[1])
     for n in range(held):
         term = jnp.dot(turned[n], whole(n, 1), preferred_element_type=jnp.float32)
         for c in range(2):

time: 58.6 us -> 58 us (0.990)
  Pallas kernels: 57 us -> 56.3 us
    pallas_call x1, Pallas kernels: 57 us -> 56.3 us  [shards(): pl.pallas_call(functools.partial(kernel, slices), out_shape=jax.ShapeDtyp...]
where the time goes in v8:
time: 58 us; the launch traced here: 57.8 us
  Pallas kernels  56.3 us (97%)
  local copies, waits for them, and re-layouts  1.47 us (3%)
    pallas_call x1, Pallas kernels, shards(): pl.pallas_call(functools.partial(kernel, slices), out_shape=jax.ShapeDtyp...  56.3 us
    unnamed x1, local copies, waits for them, and re-layouts  1.47 us

profile of v8, /device:TPU:0, one launch (start us, length us, event | category | flops | bytes accessed | tf_op | source)
XLA Modules:
  0.0 57.8 jit_solution(12214839646080565039)
XLA Ops:
  0.0 56.3 %shard_map.73 = f32[1,128,128]{2,1,0:T(8,128)} custom-call(bf16[1,1,512,1024]{3,2,1,0:T(8,128)(2,1)} %orb_hbm.1, bf16[1,1,8,512]{3,2,1,0:T(8,128)(2,1)} %occ_hbm.1, s32[1,128]{1,0:T(1,128)} %bitcast.2, bf16[7,512,512]{2,1,0:T(8,128)(2,1)} %w_hbm.1, s32[7]{0:T(128)} %bitcast.3, s32[7]{0:T(128)} %row_hbm.1, s32[7]{0:T(128)} %col_hbm.1), custom_call_target="tpu_custom_call" | custom-call | tf_op jit(solution)/shard_map/pallas_call | solution.py:375
  56.3 1.5 %copy.9 = f32[1,128,128]{2,1,0:T(8,128)} copy(f32[1,128,128]{2,1,0:T(8,128)} %shard_map.73) | data formatting | bytes 131072

commit v9 on v8

--- a/solution.py
+++ b/solution.py
@@ -299,9 +299,9 @@
         return carry
 
     lax.fori_loop(0, held, weigh, 0)
+    acc[...] = jnp.zeros_like(acc)
     arrive(fetched[0])
 
-    acc[...] = jnp.zeros_like(acc)
 
     def whole(n, i):
         parts = []

time: 58 us -> 58 us (level)
  no operation moved by 1% of the time
where the time goes in v9:
time: 58 us; the launch traced here: 57.8 us
  Pallas kernels  56.3 us (97%)
  local copies, waits for them, and re-layouts  1.47 us (3%)
    pallas_call x1, Pallas kernels, shards(): pl.pallas_call(functools.partial(kernel, slices), out_shape=jax.ShapeDtyp...  56.3 us
    unnamed x1, local copies, waits for them, and re-layouts  1.47 us

profile of v9, /device:TPU:0, one launch (start us, length us, event | category | flops | bytes accessed | tf_op | source)
XLA Modules:
  0.0 57.8 jit_solution(12672522303158130352)
XLA Ops:
  0.0 56.3 %shard_map.73 = f32[1,128,128]{2,1,0:T(8,128)} custom-call(bf16[1,1,512,1024]{3,2,1,0:T(8,128)(2,1)} %orb_hbm.1, bf16[1,1,8,512]{3,2,1,0:T(8,128)(2,1)} %occ_hbm.1, s32[1,128]{1,0:T(1,128)} %bitcast.2, bf16[7,512,512]{2,1,0:T(8,128)(2,1)} %w_hbm.1, s32[7]{0:T(128)} %bitcast.3, s32[7]{0:T(128)} %row_hbm.1, s32[7]{0:T(128)} %col_hbm.1), custom_call_target="tpu_custom_call" | custom-call | tf_op jit(solution)/shard_map/pallas_call | solution.py:375
  56.3 1.5 %copy.9 = f32[1,128,128]{2,1,0:T(8,128)} copy(f32[1,128,128]{2,1,0:T(8,128)} %shard_map.73) | data formatting | bytes 131072
